TPU v7x, 32 devices: a whole 2x2x4 slice. The times are simulated.
32 devices in a mesh: seq: 32 (over z, y, x, core).
Axes of the slice: x: 2, y: 2, z: 4, core: 2. Of those that a mesh axis runs over, the one named last changes fastest.
Arguments:
- block_input: float32 [4096, 1024], P('seq'), may hold values from -6 to 6
- cotangent: float32 [4096, 1024], P('seq'), may hold values from -6 to 6
- attn_gain: bfloat16 [1024], P('seq'), may hold values from 0.5 to 1.5
- w_query: bfloat16 [1024, 512], P('seq'), may hold values from -0.1875 to 0.1875
- w_key: bfloat16 [1024, 512], P('seq'), may hold values from -0.1875 to 0.1875
- w_value: bfloat16 [1024, 1024], P('seq'), may hold values from -0.1875 to 0.1875
- w_outgate: bfloat16 [1024, 1024], P('seq'), may hold values from -0.1875 to 0.1875
- w_decay_down: bfloat16 [1024, 16], P('seq'), may hold values from -0.1875 to 0.1875
- w_decay_up: bfloat16 [16, 512], P(None, 'seq'), may hold values from -2.5 to 2.5
- decay_bias: bfloat16 [512], P('seq')
- head_gain: bfloat16 [256], P('seq'), may hold values from 0.5 to 1.5
- w_out: bfloat16 [1024, 1024], P('seq'), may hold values from -0.1875 to 0.1875
- mlp_gain: bfloat16 [1024], P('seq'), may hold values from 0.5 to 1.5
- w_gate: bfloat16 [1024, 2816], P('seq'), may hold values from -0.1875 to 0.1875
- w_up: bfloat16 [1024, 2816], P('seq'), may hold values from -0.1875 to 0.1875
- w_down: bfloat16 [2816, 1024], P('seq'), may hold values from -0.109375 to 0.109375
Outputs:
- block_output: float32 [4096, 1024], P('seq')
- input_grad: float32 [4096, 1024], P('seq')
- grad_attn_gain: float32 [1024], P('seq')
- grad_query: float32 [1024, 512], P('seq')
- grad_key: float32 [1024, 512], P('seq')
- grad_value: float32 [1024, 1024], P('seq')
- grad_outgate: float32 [1024, 1024], P('seq')
- grad_decay_down: float32 [1024, 16], P('seq')
- grad_decay_up: float32 [16, 512], P(None, 'seq')
- grad_decay_bias: float32 [512], P('seq')
- grad_head_gain: float32 [256], P('seq')
- grad_out: float32 [1024, 1024], P('seq')
- grad_mlp_gain: float32 [1024], P('seq')
- grad_gate: float32 [1024, 2816], P('seq')
- grad_up: float32 [1024, 2816], P('seq')
- grad_down: float32 [2816, 1024], P('seq')
All inputs are finite; a program needn't handle non-finite values.
Results may differ from a plain program's by a relative error of at most 0.02.
Values may be sent and summed in bfloat16 or wider, within the bound.
No kernel may reach another device: no remote copies, remote signals or barrier semaphores. Data moves between devices by JAX's collectives and lax.ppermute only.
A program may use at most 320 MiB of HBM per device.

v0:
```python
import jax
import jax.numpy as jnp
from jax import lax
from jax.experimental import pallas as pl
from jax.experimental.pallas import tpu as pltpu
from jax.sharding import PartitionSpec as P

H = 4
DK = 128
VALUE_WIDTH = 256
GROUP = 64


EPS = 1e-05
GATE_NORM = 16.0
TOP_PRECISION = lax.Precision.HIGHEST


LANES = 128


def pack_small(pieces):
    flat = jnp.concatenate([piece.reshape(-1) for piece in pieces])
    return jnp.pad(flat, (0, -flat.shape[0] % LANES))


def pack_small_sums(pieces, devices):
    flat = jnp.concatenate([piece.reshape(devices, -1) for piece in pieces], axis=1)
    return jnp.pad(flat, ((0, 0), (0, -flat.shape[1] % LANES)))


def unpack_small(flat, shapes):
    pieces, at = [], 0
    for shape in shapes:
        size = 1
        for extent in shape:
            size *= extent
        pieces.append(flat[..., at : at + size].reshape(flat.shape[:-1] + shape))
        at += size
    return pieces


def column_slices(array, widths):
    pieces, at = [], 0
    for width in widths:
        pieces.append(array[:, at : at + width])
        at += width
    return pieces


def neighbour_ring(count):
    if count % 8:
        return tuple(range(count))
    levels, order = count // 8, []
    for column, chip in enumerate((0, 1, 3, 2)):
        climb = range(levels) if column % 2 == 0 else range(levels - 1, -1, -1)
        for level in climb:
            order += [8 * level + 2 * chip, 8 * level + 2 * chip + 1]
    return tuple(order)


def in_vmem():
    return pl.BlockSpec(memory_space=pltpu.VMEM)


def prefix_body(states, logs, out):
    count = states.shape[0]
    carried = jnp.zeros(states.shape[1:], jnp.float32)
    for device in range(count):
        out[device] = carried.astype(out.dtype)
        fading = jnp.exp(logs[device].astype(jnp.float32).sum(axis=-1, keepdims=True))
        carried = fading * carried + states[device].astype(jnp.float32)


def suffix_body(states, logs, out):
    count = states.shape[0]
    carried = jnp.zeros(states.shape[1:], jnp.float32)
    for device in range(count - 1, -1, -1):
        out[device] = carried.astype(out.dtype)
        fading = jnp.exp(logs[device].astype(jnp.float32).sum(axis=-1, keepdims=True))
        carried = fading * carried + states[device].astype(jnp.float32)


def scan_devices(body, states, logs):
    return pl.pallas_call(
        body,
        out_shape=jax.ShapeDtypeStruct(states.shape, jnp.bfloat16),
        in_specs=[in_vmem(), in_vmem()],
        out_specs=in_vmem(),
    )(states, logs)


def exchange(array):
    return lax.all_to_all(array, "seq", 0, 0)


PLANE = 8
OFFSETS = (0, 2, 4, 6)


def plane_groups(count):
    return [list(range(start, start + PLANE)) for start in range(0, count, PLANE)]


def level_groups(count):
    return [list(range(place, count, PLANE)) for place in range(PLANE)]


def swapped(array, offset):
    count = lax.axis_size("seq")
    return lax.ppermute(array, "seq", [(device, device ^ offset) for device in range(count)])


def plane_gather(array):
    same = [array] + [swapped(array, offset) for offset in OFFSETS[1:]]
    return jnp.concatenate(same + [swapped(part, 1) for part in same], axis=0)


def plane_scatter(partial):
    half = partial.shape[0] // 2
    rows = half // len(OFFSETS)
    joined = partial[:half] + swapped(partial[half:].astype(jnp.bfloat16), 1).astype(jnp.float32)
    total = joined[:rows]
    for place, offset in enumerate(OFFSETS[1:], 1):
        piece = joined[place * rows : (place + 1) * rows].astype(jnp.bfloat16)
        total = total + swapped(piece, offset).astype(jnp.float32)
    return total


def to_units(weight, levels, padded):
    rows, hidden = weight.shape
    width = hidden // (levels * PLANE)
    parts = weight.reshape(rows, levels, PLANE, width).transpose(2, 0, 1, 3)
    parts = parts.reshape(PLANE, rows, levels * width)
    return jnp.pad(parts, ((0, 0), (0, 0), (0, padded - levels * width)))


def from_units(parts, levels, hidden):
    rows = parts.shape[1]
    width = hidden // (levels * PLANE)
    parts = parts[:, :, : levels * width].reshape(PLANE, rows, levels, width)
    return parts.transpose(1, 2, 0, 3).reshape(rows, hidden)


def grad_body(left, own, other, *rest):
    out = rest[-1]
    tokens = own.shape[0]
    total = outer_sum(left[:tokens, :], own[...]) + outer_sum(left[tokens:, :], other[...])
    out[...] = total.astype(out.dtype)


def grad_into(left, right, buffer, total, start, block):
    tokens, height = left.shape
    first = start // block
    operands = [left, right, swapped(right, 1)]
    specs = [
        pl.BlockSpec((tokens, height), lambda j: (0, 0)),
        pl.BlockSpec((tokens // 2, block), lambda j: (0, j)),
        pl.BlockSpec((tokens // 2, block), lambda j: (0, j)),
    ]
    aliases = {}
    if buffer is not None:
        aliases = {len(operands): 0}
        operands.append(buffer)
        specs.append(pl.BlockSpec(memory_space=pl.ANY))
    return pl.pallas_call(
        grad_body,
        grid=(pl.cdiv(right.shape[1], block),),
        in_specs=specs,
        out_specs=pl.BlockSpec((height, block), lambda j: (0, j + first)),
        out_shape=jax.ShapeDtypeStruct((height, total), jnp.bfloat16),
        input_output_aliases=aliases,
    )(*operands)


def with_partner(array):
    return jnp.concatenate([array, swapped(array, 1)], axis=0)


def own_columns(array, chips, parity, rows):
    width = array.shape[1]
    column = jnp.arange(width // 2)
    place = jnp.asarray(chips, jnp.int32)[column // rows]
    source = (2 * place + parity) * rows + column % rows
    pick = jnp.arange(width)[:, None] == source[None, :]
    return jnp.dot(array, pick.astype(array.dtype), preferred_element_type=array.dtype)


def matmul(left_side, right_side):
    return jnp.dot(left_side, right_side, preferred_element_type=jnp.float32)


def times_back(left_side, right_side):
    return lax.dot_general(
        left_side, right_side, (((1,), (1,)), ((), ())), preferred_element_type=jnp.float32
    )


def outer_sum(left_side, right_side):
    return lax.dot_general(
        left_side, right_side, (((0,), (0,)), ((), ())), preferred_element_type=jnp.float32
    )


def rms_norm(matrix, gain):
    scaling = lax.rsqrt(jnp.mean(matrix * matrix, axis=-1, keepdims=True) + EPS)
    return matrix * scaling * gain


def swiglu(gate_pre, up_pre):
    return jax.nn.silu(gate_pre) * up_pre


def sized(left, right, contract, precision=TOP_PRECISION):
    return lax.dot_general(
        left, right, (contract, ((), ())), precision=precision, preferred_element_type=jnp.float32
    )


ROWS_BY_ROWS = ((0,), (0,))
COLUMNS_BY_COLUMNS = ((1,), (1,))
PLAIN = ((1,), (0,))


def triangle(size, lower=True):
    row = lax.broadcasted_iota(jnp.int32, (size, size), 0)
    column = lax.broadcasted_iota(jnp.int32, (size, size), 1)
    return (row >= column if lower else row <= column).astype(jnp.float32)


def log_decay_of(logit):
    return (jnp.minimum(logit, 0.0) - jnp.log1p(jnp.exp(-jnp.abs(logit)))) / GATE_NORM


def state_body(key, value, low, up, bias, logit_out, out):
    tokens, width = key.shape
    logit = sized(low[...].astype(jnp.bfloat16), up[...], PLAIN, None) + bias[...]
    logit_out[...] = logit
    log_decay = log_decay_of(logit)
    later = 1.0 - triangle(tokens)
    remaining = sized(later, log_decay, PLAIN)
    state = sized(key[...] * jnp.exp(remaining), value[...], ROWS_BY_ROWS)
    total = sized(log_decay, jnp.ones((tokens, LANES), jnp.float32), ROWS_BY_ROWS)
    high = total.astype(jnp.bfloat16).astype(jnp.float32)
    middle = (total - high).astype(jnp.bfloat16).astype(jnp.float32)
    lane = lax.broadcasted_iota(jnp.int32, (width, LANES), 1)
    pieces = jnp.where(lane == 0, high, jnp.where(lane == 1, middle, total - high - middle))
    out[:, : state.shape[1]] = state.astype(out.dtype)
    out[:, state.shape[1] :] = jnp.where(lane < 3, pieces, 0.0).astype(out.dtype)


def block_terms(query, key, log_decay):
    inner = sized(triangle(GROUP), log_decay, PLAIN)
    ending = inner[GROUP - 1 : GROUP, :]
    rising, falling = jnp.exp(inner), jnp.exp(-inner)
    fading = jnp.exp(ending - inner)
    return rising, falling, fading, query * rising, key * falling, key * fading


def ending_columns(log_decay, width):
    return jnp.exp(sized(log_decay, jnp.ones((log_decay.shape[0], width), jnp.float32), ROWS_BY_ROWS))


def output_body(query, key, value, logit, outgate, gain, entering, mixer_out, gated_out):
    state = entering[...].astype(jnp.float32)
    causal = triangle(GROUP)
    count = query.shape[0] // GROUP
    for block in range(count):
        at = slice(block * GROUP, (block + 1) * GROUP)
        log_decay = log_decay_of(logit[at, :])
        values = value[at, :]
        _, _, _, query_in, key_in, key_end = block_terms(
            query[at, :] * DK ** (-0.5), key[at, :], log_decay
        )
        scores = sized(query_in, key_in, COLUMNS_BY_COLUMNS) * causal
        mixer = sized(scores, values, PLAIN) + sized(query_in, state, PLAIN)
        if block < count - 1:
            state = ending_columns(log_decay, state.shape[1]) * state + sized(
                key_end, values, ROWS_BY_ROWS
            )
        mixer_out[at, :] = mixer
        scale = lax.rsqrt(jnp.mean(mixer * mixer, axis=-1, keepdims=True) + EPS)
        gate = outgate[at, :]
        gated_out[at, :] = (mixer * scale * gain[...] * gate * jax.nn.sigmoid(gate)).astype(
            gated_out.dtype
        )


def gate_back_body(
    d_gated, mixer, outgate, gain, query, logit, d_mixer_out, d_gate_out, gain_out, state_out
):
    tokens = query.shape[0]
    scale = lax.rsqrt(jnp.mean(mixer[...] * mixer[...], axis=-1, keepdims=True) + EPS)
    unit = mixer[...] * scale
    sigmoid = jax.nn.sigmoid(outgate[...])
    gradient = d_gated[...] * outgate[...] * sigmoid
    inward = gradient * gain[...]
    d_mixer = scale * (inward - unit * jnp.mean(inward * unit, axis=-1, keepdims=True))
    d_mixer_out[...] = d_mixer
    d_gate = d_gated[...] * unit * gain[...] * sigmoid * (1.0 + outgate[...] * (1.0 - sigmoid))
    d_gate_out[...] = d_gate.astype(d_gate_out.dtype)

    @pl.when(pl.program_id(0) == 0)
    def _():
        gain_out[...] = jnp.zeros(gain_out.shape, jnp.float32)

    gain_out[...] += jnp.sum(gradient * unit, axis=0, keepdims=True)
    cumulative = sized(triangle(tokens), log_decay_of(logit[...]), PLAIN)
    state_out[...] = sized(
        query[...] * (DK ** (-0.5)) * jnp.exp(cumulative), d_mixer, ROWS_BY_ROWS
    ).astype(state_out.dtype)


def mixer_back_body(
    query, key, value, logit, d_mixer, entering, leaving, d_gate, up, out, d_logit_out, bias_out, low
):
    head = pl.program_id(0)
    heads = pl.num_programs(0)
    width, value_width = key.shape[1], value.shape[1]
    count = query.shape[0] // GROUP
    causal, upper = triangle(GROUP), triangle(GROUP, lower=False)
    ones = jnp.ones((8, value_width), jnp.float32)
    state, blocks = entering[...].astype(jnp.float32), []
    for block in range(count):
        at = slice(block * GROUP, (block + 1) * GROUP)
        log_decay = log_decay_of(logit[at, :])
        terms = block_terms(query[at, :] * DK ** (-0.5), key[at, :], log_decay)
        factor = ending_columns(log_decay, value_width)
        blocks.append((at, terms, factor, state))
        if block < count - 1:
            state = factor * state + sized(terms[5], value[at, :], ROWS_BY_ROWS)
    d_state = leaving[...].astype(jnp.float32)
    bias_sum = jnp.zeros((1, width), jnp.float32)
    for at, terms, factor, state in reversed(blocks):
        rising, falling, fading, query_in, key_in, key_end = terms
        values, d_out = value[at, :], d_mixer[at, :]
        scores = sized(query_in, key_in, COLUMNS_BY_COLUMNS) * causal
        d_scores = sized(d_out, values, COLUMNS_BY_COLUMNS) * causal
        d_query_in = sized(d_scores, key_in, PLAIN) + sized(d_out, state, COLUMNS_BY_COLUMNS)
        d_key_in = sized(d_scores, query_in, ROWS_BY_ROWS)
        d_values = sized(scores, d_out, ROWS_BY_ROWS) + sized(key_end, d_state, PLAIN)
        d_key_end = sized(values, d_state, COLUMNS_BY_COLUMNS)
        d_ending = sized(ones, d_state * factor * state, COLUMNS_BY_COLUMNS)[0:1, :]
        end_part = d_key_end * key_end
        d_ending = d_ending + jnp.sum(end_part, axis=0, keepdims=True)
        d_inner = d_query_in * query_in - d_key_in * key_in - end_part
        d_log_decay = sized(upper, d_inner, PLAIN) + d_ending
        d_logit = d_log_decay * jax.nn.sigmoid(-logit[at, :]) / GATE_NORM
        bias_sum = bias_sum + jnp.sum(d_logit, axis=0, keepdims=True)
        d_logit_in = d_logit.astype(jnp.bfloat16)
        d_logit_out[at, :] = d_logit_in
        d_low = sized(d_logit_in, up[...], COLUMNS_BY_COLUMNS, None)
        d_low = jnp.where(head == 0, d_low, d_low + low[at, :])
        low[at, :] = d_low
        d_state = factor * d_state + sized(query_in, d_out, ROWS_BY_ROWS)
        at_query = pl.multiple_of(head * width, width)
        at_key = pl.multiple_of((heads + head) * width, width)
        at_value = pl.multiple_of(2 * heads * width + head * value_width, value_width)
        at_gate = pl.multiple_of(2 * heads * width + (heads + head) * value_width, value_width)
        at_low = 2 * heads * (width + value_width)
        out[at, pl.ds(at_query, width)] = (DK ** (-0.5) * d_query_in * rising).astype(out.dtype)
        out[at, pl.ds(at_key, width)] = (d_key_in * falling + d_key_end * fading).astype(out.dtype)
        out[at, pl.ds(at_value, value_width)] = d_values.astype(out.dtype)
        out[at, pl.ds(at_gate, value_width)] = d_gate[at, :]
        out[at, at_low:] = d_low.astype(out.dtype)
    bias_out[...] = bias_sum


def per_head(rows, columns, offset=0):
    return pl.BlockSpec((rows, columns), lambda head: (0, head + offset))


def per_head_rows(rows, columns):
    return pl.BlockSpec((rows, columns), lambda head: (head, 0))


def whole_at(rows, columns, place):
    return pl.BlockSpec((rows, columns), lambda head: (0, place))


def whole(rows, columns):
    return pl.BlockSpec((rows, columns), lambda head: (0, 0))


def local(
    block_input,
    cotangent,
    attn_gain,
    w_query,
    w_key,
    w_value,
    w_outgate,
    w_decay_down,
    w_decay_up,
    decay_bias,
    head_gain,
    w_out,
    mlp_gain,
    w_gate,
    w_up,
    w_down,
):
    count = lax.axis_size("seq")
    rows = w_query.shape[0]
    key_width, value_width, rank = (w_query.shape[1], w_value.shape[1], w_decay_down.shape[1])
    hidden = w_gate.shape[1]
    small_shapes = (w_decay_up.shape, attn_gain.shape, mlp_gain.shape, decay_bias.shape, head_gain.shape)
    first = jnp.concatenate(
        [
            w_query,
            w_key,
            w_value,
            w_outgate,
            jnp.pad(w_decay_down, ((0, 0), (0, LANES - rank))),
            w_out,
        ],
        axis=1,
    )
    small = pack_small((w_decay_up, attn_gain, mlp_gain, decay_bias, head_gain))
    small = exchange(jnp.broadcast_to(small, (count, 1) + small.shape)).reshape(count, -1)
    first = lax.all_gather(first, "seq", axis=0, tiled=True)
    levels = count // PLANE
    planes, columns = (plane_groups(count), level_groups(count))
    units = levels * w_down.shape[0]
    padded = -(-units // LANES) * LANES
    gate_up = jnp.concatenate([to_units(w_gate, levels, padded), to_units(w_up, levels, padded)], axis=2)
    gate_up = lax.all_to_all(gate_up, "seq", 0, 0, axis_index_groups=planes)
    gate_up = gate_up.reshape(PLANE * rows, 2 * padded)
    gate_up = lax.all_gather(gate_up, "seq", axis=0, tiled=True, axis_index_groups=columns)
    down = lax.all_gather(w_down, "seq", axis=0, tiled=True, axis_index_groups=columns)
    down = jnp.pad(down, ((0, padded - units), (0, 0)))
    cot_in, first = lax.optimization_barrier((cotangent.astype(jnp.bfloat16), first))
    cot_plane = plane_gather(cot_in)
    widths = (key_width, key_width, value_width, value_width)
    wide = 2 * key_width + 2 * value_width
    projection = first[:, : wide + LANES]
    up_pieces, attn_full, mlp_full_gain, bias_full, head_full = unpack_small(small, small_shapes)
    decay_up_full = up_pieces.transpose(1, 0, 2).reshape(rank, key_width)
    attn_full, mlp_full_gain, bias_full, head_full = (
        piece.reshape(-1).astype(jnp.float32) for piece in (attn_full, mlp_full_gain, bias_full, head_full)
    )
    out_full = first[:, wide + LANES :]
    scaling = DK ** (-0.5)
    normed, norm_back = jax.vjp(rms_norm, block_input, attn_full)
    normed_in = normed.astype(jnp.bfloat16)
    wide_out = matmul(normed_in, projection)
    tokens = wide_out.shape[0]
    up_rows = jnp.pad(decay_up_full, ((0, LANES - rank), (0, 0)))
    value_at = 2 * key_width // VALUE_WIDTH
    query_spec, key_spec = per_head(tokens, DK), per_head(tokens, DK, H)
    value_spec = per_head(tokens, VALUE_WIDTH, value_at)
    gate_spec = per_head(tokens, VALUE_WIDTH, value_at + H)
    low_spec = whole_at(tokens, LANES, wide // LANES)
    up_spec = per_head(LANES, DK)
    head_values, head_keys = per_head(tokens, VALUE_WIDTH), per_head(tokens, DK)
    state_spec = per_head_rows(DK, VALUE_WIDTH)
    gain_spec = whole(1, VALUE_WIDTH)
    gain_row = head_full[None, :]
    chunk = key_width // count
    decay_logit, outgoing = pl.pallas_call(
        state_body,
        grid=(H,),
        in_specs=[key_spec, value_spec, low_spec, up_spec, per_head(1, DK)],
        out_specs=[head_keys, per_head_rows(DK, VALUE_WIDTH + LANES)],
        out_shape=[
            jax.ShapeDtypeStruct((tokens, key_width), jnp.float32),
            jax.ShapeDtypeStruct((key_width, VALUE_WIDTH + LANES), jnp.bfloat16),
        ],
    )(wide_out, wide_out, wide_out, up_rows, bias_full[None, :])
    arrived = exchange(outgoing.reshape(count, chunk, VALUE_WIDTH + LANES))
    logs = arrived[:, :, VALUE_WIDTH:]
    before = exchange(scan_devices(prefix_body, arrived[:, :, :VALUE_WIDTH], logs))
    before = before.reshape(key_width, VALUE_WIDTH)
    mixer, gated = pl.pallas_call(
        output_body,
        grid=(H,),
        in_specs=[query_spec, key_spec, value_spec, head_keys, gate_spec, gain_spec, state_spec],
        out_specs=[head_values, head_values],
        out_shape=[
            jax.ShapeDtypeStruct((tokens, value_width), jnp.float32),
            jax.ShapeDtypeStruct((tokens, value_width), jnp.bfloat16),
        ],
    )(wide_out, wide_out, wide_out, decay_logit, wide_out, gain_row, before)
    hidden_state = block_input + matmul(gated, out_full)
    mlp_full, mlp_back = jax.vjp(rms_norm, hidden_state, mlp_full_gain)
    mlp_normed = mlp_full.astype(jnp.bfloat16)
    mlp_plane = plane_gather(mlp_normed)
    gate_pre, up_pre = column_slices(matmul(mlp_plane, gate_up), (padded, padded))
    activ_full, activ_back = jax.vjp(swiglu, gate_pre, up_pre)
    activ = activ_full.astype(jnp.bfloat16)
    d_activ = times_back(cot_plane, down)
    d_gate_full, d_up_full = activ_back(d_activ)
    d_gate_up = jnp.concatenate(
        [d_gate_full.astype(jnp.bfloat16), d_up_full.astype(jnp.bfloat16)], axis=1
    )
    d_mlp_normed = plane_scatter(times_back(d_gate_up, gate_up))

    def level_sum(partial):
        return lax.psum_scatter(
            partial.astype(jnp.bfloat16),
            "seq",
            scatter_dimension=0,
            tiled=True,
            axis_index_groups=columns,
        )

    sum_down = level_sum(outer_sum(activ, cot_plane)[:units]).astype(jnp.float32)
    sum_gate_up = level_sum(outer_sum(mlp_plane, d_gate_up)).reshape(PLANE, rows, 2 * padded)
    sum_gate_up = lax.all_to_all(sum_gate_up, "seq", 0, 0, axis_index_groups=planes)
    sum_gate_up = sum_gate_up.astype(jnp.float32)
    sum_gate = from_units(sum_gate_up[:, :, :padded], levels, hidden)
    sum_up_proj = from_units(sum_gate_up[:, :, padded:], levels, hidden)
    d_hidden_norm, grad_mlp_gain = mlp_back(d_mlp_normed)
    d_hidden = cotangent + d_hidden_norm
    d_hidden_in = d_hidden.astype(jnp.bfloat16)
    d_gated = times_back(d_hidden_in, out_full)
    mixer_gradient, d_outgate, grad_head_gain, state_gradient = pl.pallas_call(
        gate_back_body,
        grid=(H,),
        in_specs=[head_values, head_values, gate_spec, gain_spec, query_spec, head_keys],
        out_specs=[head_values, head_values, gain_spec, state_spec],
        out_shape=[
            jax.ShapeDtypeStruct((tokens, value_width), jnp.float32),
            jax.ShapeDtypeStruct((tokens, value_width), jnp.bfloat16),
            jax.ShapeDtypeStruct((1, VALUE_WIDTH), jnp.float32),
            jax.ShapeDtypeStruct((key_width, VALUE_WIDTH), jnp.bfloat16),
        ],
    )(d_gated, mixer, wide_out, gain_row, wide_out, decay_logit)
    arrived_back = exchange(state_gradient.reshape(count, chunk, VALUE_WIDTH))
    after = exchange(scan_devices(suffix_body, arrived_back, logs))
    activ_late, after = lax.optimization_barrier((activ, after))
    block_output = hidden_state + plane_scatter(matmul(activ_late, down))
    after = after.reshape(key_width, VALUE_WIDTH)
    d_first, d_logit_in, grad_decay_bias = pl.pallas_call(
        mixer_back_body,
        grid=(H,),
        in_specs=[
            query_spec,
            key_spec,
            value_spec,
            head_keys,
            head_values,
            state_spec,
            state_spec,
            head_values,
            up_spec,
        ],
        out_specs=[whole(tokens, wide + LANES), head_keys, per_head(1, DK)],
        out_shape=[
            jax.ShapeDtypeStruct((tokens, wide + LANES), jnp.bfloat16),
            jax.ShapeDtypeStruct((tokens, key_width), jnp.bfloat16),
            jax.ShapeDtypeStruct((1, key_width), jnp.float32),
        ],
        scratch_shapes=[pltpu.VMEM((tokens, LANES), jnp.float32)],
    )(
        wide_out,
        wide_out,
        wide_out,
        decay_logit,
        mixer_gradient,
        before,
        after,
        d_outgate,
        up_rows,
    )
    low_rank = wide_out[:, wide : wide + rank].astype(jnp.bfloat16)
    grad_decay_up = outer_sum(low_rank, d_logit_in)
    d_normed = times_back(d_first, projection)
    d_input_norm, grad_attn_gain = norm_back(d_normed)
    input_grad = d_hidden + d_input_norm

    small_sums = pack_small_sums(
        (
            grad_decay_up.reshape(rank, count, -1).transpose(1, 0, 2),
            grad_attn_gain,
            grad_mlp_gain,
            grad_decay_bias,
            grad_head_gain.reshape(-1),
        ),
        count,
    )
    small_sums = jnp.sum(exchange(small_sums), axis=0)
    order = neighbour_ring(count)
    chips = tuple(device // 2 for device in order[::2])
    rings = [[2 * chip + core for chip in chips] for core in range(2)]
    parity = lax.axis_index("seq") % 2
    normed_pair = own_columns(with_partner(normed_in), chips, parity, rows)
    gated_pair = own_columns(with_partner(gated), chips, parity, rows)
    width = wide + LANES + w_out.shape[1]
    sums = grad_into(gated_pair, d_hidden_in, None, width, wide + LANES, LANES)
    sums = grad_into(normed_pair, d_first, sums, width, 0, 640)
    sums = lax.psum_scatter(
        sums, "seq", scatter_dimension=0, tiled=True, axis_index_groups=rings
    ).astype(jnp.float32)
    sum_first, sum_out = column_slices(sums, (wide + LANES, w_out.shape[1]))
    sum_query, sum_key, sum_value, sum_outgate, sum_decay_down = column_slices(
        sum_first, widths + (rank,)
    )
    sum_up, sum_attn, sum_mlp, sum_bias, sum_head = unpack_small(
        small_sums, small_shapes
    )
    return (
        block_output,
        input_grad,
        sum_attn,
        sum_query,
        sum_key,
        sum_value,
        sum_outgate,
        sum_decay_down,
        sum_up,
        sum_bias,
        sum_head,
        sum_out,
        sum_mlp,
        sum_gate,
        sum_up_proj,
        sum_down,
    )


def solution(mesh):
    return jax.shard_map(
        local,
        mesh=mesh,
        in_specs=(
            P("seq", None),
            P("seq", None),
            P("seq"),
            P("seq", None),
            P("seq", None),
            P("seq", None),
            P("seq", None),
            P("seq", None),
            P(None, "seq"),
            P("seq"),
            P("seq"),
            P("seq", None),
            P("seq"),
            P("seq", None),
            P("seq", None),
            P("seq", None),
        ),
        out_specs=(
            P("seq", None),
            P("seq", None),
            P("seq"),
            P("seq", None),
            P("seq", None),
            P("seq", None),
            P("seq", None),
            P("seq", None),
            P(None, "seq"),
            P("seq"),
            P("seq"),
            P("seq", None),
            P("seq"),
            P("seq", None),
            P("seq", None),
            P("seq", None),
        ),
        check_vma=False,
    )
```

profile of v0, /device:TPU:0, one launch (start us, length us, event | category | flops | bytes accessed | tf_op | source)
XLA Modules:
  0.0 396.3 jit_solution(10726788171735632259)
XLA Ops:
  19.3 7.3 %all-to-all-start = ((bf16[32,2,192]{2,1,0:T(2,128)(2,1)}), bf16[32,2,192]{2,1,0:T(2,128)(2,1)S(1)}, u32[]{:S(2)}, u32[]{:S(2)}) async-start(bf16[32,2,192]{2,1,0:T(2,128)(2,1)} %reshape.383), calls=%async_computation | async-start | bytes 65536 | tf_op jit(solution)/shard_map/all_to_all | solution.py:94
  39.8 55.2 %all-gather.3.cloned.1.call-done = bf16[1024,4224]{1,0:T(8,128)(2,1)} async-done(((bf16[32,4224]{1,0:T(8,128)(2,1)}), bf16[1024,4224]{1,0:T(8,128)(2,1)}) %all-gather.3.cloned.1.call-update) | async-done | bytes 8650768 | tf_op jit(solution)/shard_map/all_gather | solution.py:421
  95.1 5.1 %fusion.2.key.value.low.query.outgate = f32[128,3200]{1,0:T(8,128)} fusion(bf16[128,1024]{1,0:T(8,128)(2,1)S(1)} %multiply_convert_fusion.3, bf16[1024,4224]{1,0:T(8,128)(2,1)} %all-gather.3.cloned.1.call-done), kind=kOutput, calls=%fused_computation.2 | convolution fusion | flops 838860800 | bytes 8454144 | tf_op jit(solution)/shard_map/dot_general | solution.py:190
  100.2 5.1 %shard_map.297 = (f32[128,512]{1,0:T(8,128)}, bf16[512,384]{1,0:T(8,128)(2,1)}) custom-call(f32[128,3200]{1,0:T(8,128)} %fusion.2.key.value.low.query.outgate, f32[128,3200]{1,0:T(8,128)} %fusion.2.key.value.low.query.outgate, f32[128,3200]{1,0:T(8,128)} %fusion.2.key.value.low.query.outgate, bf16[128,512]{1,0:T(8,128)(2,1)} %pad.29.up, f32[1,512]{1,0:T(1,128)} %reshape.287.bias), custom_call_target="tpu_custom_call" | custom-call | tf_op jit(solution)/shard_map/pallas_call | solution.py:460
  108.7 23.8 %all_gather.11 = bf16[352,1024]{1,0:T(8,128)(2,1)S(1)} all-gather(bf16[88,1024]{1,0:T(8,128)(2,1)S(1)} %copy-done.19), channel_id=1, replica_groups={{0,8,16,24},{1,9,17,25},{2,10,18,26},{3,11,19,27},{4,12,20,28},{5,13,21..., dimensions={0}, use_global_device_ids=true | all-gather | bytes 901120 | tf_op jit(solution)/shard_map/all_gather | solution.py:430
  140.2 5.9 %all-to-all-start.2 = ((bf16[32,16,256]{2,1,0:T(8,128)(2,1)}), bf16[32,16,256]{2,1,0:T(8,128)(2,1)S(1)}, u32[]{:S(2)}, u32[]{:S(2)}) async-start(bf16[32,16,256]{2,1,0:T(8,128)(2,1)} %shard_map.298), calls=%async_computation.2 | async-start | bytes 524288 | tf_op jit(solution)/shard_map/all_to_all | solution.py:94
  150.8 11.9 %all-to-all-done.2 = bf16[32,16,256]{2,1,0:T(8,128)(2,1)S(1)} async-done(((bf16[32,16,256]{2,1,0:T(8,128)(2,1)}), bf16[32,16,256]{2,1,0:T(8,128)(2,1)S(1)}, u32[]{:S(2)}, u32[]{:S(2)}) %all-to-all-start.2) | async-done | bytes 262176 | tf_op jit(solution)/shard_map/all_to_all | solution.py:94
  163.4 7.0 %shard_map.299 = (f32[128,1024]{1,0:T(8,128)}, bf16[128,1024]{1,0:T(8,128)(2,1)}) custom-call(f32[128,3200]{1,0:T(8,128)} %fusion.2.key.value.low.query.outgate, f32[128,3200]{1,0:T(8,128)} %fusion.2.key.value.low.query.outgate, f32[128,3200]{1,0:T(8,128)} %fusion.2.key.value.low.query.outgate, f32[128,512]{1,0:T(8,128)} %get-tuple-element.32.logit, ...), custom_call_target="tpu_custom_call" | custom-call | tf_op jit(solution)/shard_map/pallas_call | solution.py:474
  183.6 4.4 %collective-permute-done.1 = bf16[128,1024]{1,0:T(8,128)(2,1)S(1)} collective-permute-done((bf16[128,1024]{1,0:T(8,128)(2,1)S(1)}, bf16[128,1024]{1,0:T(8,128)(2,1)S(1)}, u32[]{:S(2)}, u32[]{:S(2)}) %collective-permute-start.1) | collective-permute-done | bytes 262176 | tf_op jit(solution)/shard_map/ppermute | solution.py:111
  193.5 3.9 fusion.66
  203.0 3.8 fusion.67
  214.7 4.6 %convolution_convert_fusion = bf16[1024,768]{1,0:T(8,128)(2,1)} fusion(bf16[1024,1024]{1,0:T(8,128)(2,1)} %constant_dynamic-update-slice_fusion.6, bf16[1024,384]{0,1:T(8,128)(2,1)S(1)} %copy-done.27, bf16[1024,384]{0,1:T(8,128)(2,1)S(1)} %copy-done.25), kind=kOutput, calls=%fused_computation.16 | convolution fusion | flops 1614544896 | bytes 5242880 | tf_op jit(solution)/shard_map/dot_general | solution.py:200
  220.6 5.8 %collective-permute-done.17 = bf16[128,1024]{1,0:T(8,128)(2,1)} collective-permute-done((bf16[128,1024]{1,0:T(8,128)(2,1)}, bf16[128,1024]{1,0:T(8,128)(2,1)}, u32[]{:S(2)}, u32[]{:S(2)}) %collective-permute-start.17) | collective-permute-done | bytes 262176 | tf_op jit(solution)/shard_map/ppermute | solution.py:111
  232.5 5.5 %shard_map.300 = (f32[128,1024]{1,0:T(8,128)}, bf16[128,1024]{1,0:T(8,128)(2,1)}, f32[1,256]{1,0:T(1,128)}, bf16[512,256]{1,0:T(8,128)(2,1)}) custom-call(f32[128,1024]{1,0:T(8,128)} %fusion.6.d_gated, f32[128,1024]{1,0:T(8,128)} %get-tuple-element.36.mixer, f32[128,3200]{1,0:T(8,128)} %fusion.2.key.value.low.query.outgate, f32[1,256]{1,0:T(1,128)} %reshape.288.gain, ...), custom_call_target="tpu_custom_call" | custom-call | tf_op jit(solution)/shard_map/pallas_call | solution.py:517
  238.0 20.1 %all_to_all.44.states = bf16[32,16,256]{2,1,0:T(8,128)(2,1)} all-to-all(bf16[32,16,256]{2,1,0:T(8,128)(2,1)} %bitcast.59), channel_id=1, replica_groups=mesh['seq'=32] {'seq'}, dimensions={0} | all-to-all | bytes 524288 | tf_op jit(solution)/shard_map/all_to_all | solution.py:94
  259.9 16.7 %all_to_all.45 = bf16[32,16,256]{2,1,0:T(8,128)(2,1)} all-to-all(bf16[32,16,256]{2,1,0:T(8,128)(2,1)} %shard_map.301), channel_id=1, replica_groups=mesh['seq'=32] {'seq'}, dimensions={0} | all-to-all | bytes 524288 | tf_op jit(solution)/shard_map/all_to_all | solution.py:94
  276.7 11.9 %shard_map.302 = (bf16[128,3200]{1,0:T(8,128)(2,1)}, bf16[128,512]{1,0:T(8,128)(2,1)}, f32[1,512]{1,0:T(1,128)}) custom-call(f32[128,3200]{1,0:T(8,128)} %fusion.2.key.value.low.query.outgate, f32[128,3200]{1,0:T(8,128)} %fusion.2.key.value.low.query.outgate, f32[128,3200]{1,0:T(8,128)} %fusion.2.key.value.low.query.outgate, ...), custom_call_target="tpu_custom_call" | custom-call | tf_op jit(solution)/shard_map/pallas_call | solution.py:534
  296.9 5.9 %shard_map.303.rest_0_ = bf16[512,4224]{1,0:T(8,128)(2,1)} custom-call(bf16[256,512]{1,0:T(8,128)(2,1)} %fusion.4.left, bf16[128,1024]{1,0:T(8,128)(2,1)} %copy-done.11, bf16[128,1024]{1,0:T(8,128)(2,1)} %copy-done.15), custom_call_target="tpu_custom_call" | custom-call | tf_op jit(solution)/shard_map/pallas_call | solution.py:166
  303.6 6.1 %shard_map.304 = bf16[512,4224]{1,0:T(8,128)(2,1)} custom-call(bf16[256,512]{1,0:T(8,128)(2,1)} %fusion.5.left, bf16[128,3200]{1,0:T(8,128)(2,1)} %get-tuple-element.42.own, bf16[128,3200]{1,0:T(8,128)(2,1)} %copy-done.13, bf16[512,4224]{1,0:T(8,128)(2,1)} %shard_map.303.rest_0_), custom_call_target="tpu_custom_call", output_to_operand_aliasing={{}: (3, {})} | custom-call | tf_op jit(solution)/shard_map/pallas_call | solution.py:166
  317.9 6.0 %multiply_reduce_fusion.1 = (f32[1024]{0:T(1024)S(1)}, f32[128]{0:T(128)S(1)}, f32[128,1024]{1,0:T(8,128)}) fusion(f32[128,1024]{1,0:T(8,128)S(1)} %copy-done.1, f32[128]{0:T(128)S(1)} %fusion.47, f32[1024]{0:T(1024)S(1)} %reshape.286, bf16[128,3200]{1,0:T(8,128)(2,1)S(1)} %copy-done.12, bf16[1024,4224]{1,0:T(8,128)(2,1)} %all-gather.3.cloned.1.call-done), kind=kOutput, calls=%fused_computation.58 | convolution fusion | flops 839646080 | bytes 8430592 | tf_op jit(solution)/shard_map/dot_general | solution.py:194
  330.8 5.7 %all-to-all-done.6 = f32[32,1,384]{2,1,0:T(1,128)S(1)} async-done(((f32[32,1,384]{2,1,0:T(1,128)}), f32[32,1,384]{2,1,0:T(1,128)S(1)}, u32[]{:S(2)}, u32[]{:S(2)}) %all-to-all-start.6) | async-done | bytes 49184 | tf_op jit(solution)/shard_map/all_to_all | solution.py:94
  336.6 3.7 all-to-all-start.7
  359.7 7.4 %collective-permute-done.20 = bf16[128,1024]{1,0:T(8,128)(2,1)} collective-permute-done((bf16[128,1024]{1,0:T(8,128)(2,1)}, bf16[128,1024]{1,0:T(8,128)(2,1)}, u32[]{:S(2)}, u32[]{:S(2)}) %collective-permute-start.20) | collective-permute-done | bytes 262176 | tf_op jit(solution)/shard_map/ppermute | solution.py:111
  369.2 15.0 %reduce-scatter.4.cloned.1.call-done = bf16[32,4224]{1,0:T(8,128)(2,1)} async-done(((bf16[512,4224]{1,0:T(8,128)(2,1)}), bf16[32,4224]{1,0:T(8,128)(2,1)}) %reduce-scatter.4.cloned.1.call-update) | async-done | bytes 270352 | tf_op jit(solution)/shard_map/reduce_scatter | solution.py:592
  (251 shorter events, 132.1 us)
Async XLA Ops:
  8.0 87.0 %all-gather.3.cloned.1.call-start = ((), (), s32[]{:S(2)}) async-start(), calls=%async_computation.11 | async-start | bytes 8921088 | tf_op jit(solution)/shard_map/all_gather | solution.py:421
  19.3 14.8 %all-to-all-start = ((bf16[32,2,192]{2,1,0:T(2,128)(2,1)}), bf16[32,2,192]{2,1,0:T(2,128)(2,1)S(1)}, u32[]{:S(2)}, u32[]{:S(2)}) async-start(bf16[32,2,192]{2,1,0:T(2,128)(2,1)} %reshape.383), calls=%async_computation | async-start | bytes 65536 | tf_op jit(solution)/shard_map/all_to_all | solution.py:94
  34.1 71.3 %all-to-all-start.3 = ((bf16[8,32,768]{2,1,0:T(8,128)(2,1)}), bf16[8,32,768]{2,1,0:T(8,128)(2,1)S(1)}, u32[]{:S(2)}, u32[]{:S(2)}) async-start(bf16[8,32,768]{2,1,0:T(8,128)(2,1)} %fusion.39), calls=%async_computation.3 | async-start | bytes 786432 | tf_op jit(solution)/shard_map/all_to_all | solution.py:427
  105.4 31.6 %all-to-all-start.1 = ((bf16[32,16,384]{2,1,0:T(8,128)(2,1)}), bf16[32,16,384]{2,1,0:T(8,128)(2,1)S(1)}, u32[]{:S(2)}, u32[]{:S(2)}) async-start(bf16[32,16,384]{2,1,0:T(8,128)(2,1)} %bitcast.53), calls=%async_computation.1 | async-start | bytes 786432 | tf_op jit(solution)/shard_map/all_to_all | solution.py:94
  108.6 84.9 %all-gather.5.cloned.1.call-start = ((), (), s32[]{:S(2)}) async-start(), calls=%async_computation.12 | async-start | bytes 1966080 | tf_op jit(solution)/shard_map/all_gather | solution.py:429
  132.5 14.6 %collective-permute-start.9 = (bf16[128,1024]{1,0:T(8,128)(2,1)S(1)}, bf16[128,1024]{1,0:T(8,128)(2,1)S(1)}, u32[]{:S(2)}, u32[]{:S(2)}) collective-permute-start(bf16[128,1024]{1,0:T(8,128)(2,1)S(1)} %convert_element_type.131), channel_id=1, source_target_pairs={{0,6},{1,7},{2,4},{3,5},{4,2},{5,3},{6,0},{7,1},{8,14},{9,15},{10,... | collective-permute-start | bytes 786440 | tf_op jit(solution)/shard_map/ppermute | solution.py:111
  134.8 12.5 %collective-permute-start.8 = (bf16[128,1024]{1,0:T(8,128)(2,1)S(1)}, bf16[128,1024]{1,0:T(8,128)(2,1)S(1)}, u32[]{:S(2)}, u32[]{:S(2)}) collective-permute-start(bf16[128,1024]{1,0:T(8,128)(2,1)S(1)} %convert_element_type.131), channel_id=1, source_target_pairs={{0,4},{1,5},{2,6},{3,7},{4,0},{5,1},{6,2},{7,3},{8,12},{9,13},{10,... | collective-permute-start | bytes 786440 | tf_op jit(solution)/shard_map/ppermute | solution.py:111
  136.9 13.1 %collective-permute-start.10 = (bf16[128,1024]{1,0:T(8,128)(2,1)S(1)}, bf16[128,1024]{1,0:T(8,128)(2,1)S(1)}, u32[]{:S(2)}, u32[]{:S(2)}) collective-permute-start(bf16[128,1024]{1,0:T(8,128)(2,1)S(1)} %convert_element_type.131), channel_id=1, source_target_pairs={{0,1},{1,0},{2,3},{3,2},{4,5},{5,4},{6,7},{7,6},{8,9},{9,8},{10,11... | collective-permute-start | bytes 786440 | tf_op jit(solution)/shard_map/ppermute | solution.py:111
  140.2 22.5 %all-to-all-start.2 = ((bf16[32,16,256]{2,1,0:T(8,128)(2,1)}), bf16[32,16,256]{2,1,0:T(8,128)(2,1)S(1)}, u32[]{:S(2)}, u32[]{:S(2)}) async-start(bf16[32,16,256]{2,1,0:T(8,128)(2,1)} %shard_map.298), calls=%async_computation.2 | async-start | bytes 524288 | tf_op jit(solution)/shard_map/all_to_all | solution.py:94
  146.1 165.1 %reduce-scatter.8.cloned.1.call-start = ((), (), s32[]{:S(2)}) async-start(), calls=%async_computation.15 | async-start | bytes 901120 | tf_op jit(solution)/shard_map/reduce_scatter | solution.py:499
  147.1 33.2 %collective-permute-start.13 = (bf16[128,1024]{1,0:T(8,128)(2,1)S(1)}, bf16[128,1024]{1,0:T(8,128)(2,1)S(1)}, u32[]{:S(2)}, u32[]{:S(2)}) collective-permute-start(bf16[128,1024]{1,0:T(8,128)(2,1)S(1)} %collective-permute-done.9), channel_id=1, source_target_pairs={{0,1},{1,0},{2,3},{3,2},{4,5},{5,4},{6,7},{7,6},{8,9},{9,8},{10,11... | collective-permute-start | bytes 786440 | tf_op jit(solution)/shard_map/ppermute | solution.py:111
  147.3 31.3 %collective-permute-start.12 = (bf16[128,1024]{1,0:T(8,128)(2,1)S(1)}, bf16[128,1024]{1,0:T(8,128)(2,1)}, u32[]{:S(2)}, u32[]{:S(2)}) collective-permute-start(bf16[128,1024]{1,0:T(8,128)(2,1)S(1)} %collective-permute-done.8), channel_id=1, source_target_pairs={{0,1},{1,0},{2,3},{3,2},{4,5},{5,4},{6,7},{7,6},{8,9},{9,8},{10,11... | collective-permute-start | bytes 786440 | tf_op jit(solution)/shard_map/ppermute | solution.py:111
  147.6 28.8 %collective-permute-start.11 = (bf16[128,1024]{1,0:T(8,128)(2,1)S(1)}, bf16[128,1024]{1,0:T(8,128)(2,1)}, u32[]{:S(2)}, u32[]{:S(2)}) collective-permute-start(bf16[128,1024]{1,0:T(8,128)(2,1)S(1)} %collective-permute-done.7), channel_id=1, source_target_pairs={{0,1},{1,0},{2,3},{3,2},{4,5},{5,4},{6,7},{7,6},{8,9},{9,8},{10,11... | collective-permute-start | bytes 786440 | tf_op jit(solution)/shard_map/ppermute | solution.py:111
  175.9 12.1 %collective-permute-start.1 = (bf16[128,1024]{1,0:T(8,128)(2,1)S(1)}, bf16[128,1024]{1,0:T(8,128)(2,1)S(1)}, u32[]{:S(2)}, u32[]{:S(2)}) collective-permute-start(bf16[128,1024]{1,0:T(8,128)(2,1)S(1)} %get-tuple-element.122), channel_id=1, source_target_pairs={{0,4},{1,5},{2,6},{3,7},{4,0},{5,1},{6,2},{7,3},{8,12},{9,13},{10,... | collective-permute-start | bytes 786440 | tf_op jit(solution)/shard_map/ppermute | solution.py:111
  207.8 128.8 %reduce-scatter.6.cloned.1.call-start = ((), (), s32[]{:S(2)}) async-start(), calls=%async_computation.14 | async-start | bytes 1966080 | tf_op jit(solution)/shard_map/reduce_scatter | solution.py:499
  212.8 13.6 %collective-permute-start.17 = (bf16[128,1024]{1,0:T(8,128)(2,1)}, bf16[128,1024]{1,0:T(8,128)(2,1)}, u32[]{:S(2)}, u32[]{:S(2)}) collective-permute-start(bf16[128,1024]{1,0:T(8,128)(2,1)} %get-tuple-element.130), channel_id=1, source_target_pairs={{0,6},{1,7},{2,4},{3,5},{4,2},{5,3},{6,0},{7,1},{8,14},{9,15},{10,... | collective-permute-start | bytes 786440 | tf_op jit(solution)/shard_map/ppermute | solution.py:111
  214.2 13.6 %collective-permute-start.16 = (bf16[128,1024]{1,0:T(8,128)(2,1)}, bf16[128,1024]{1,0:T(8,128)(2,1)}, u32[]{:S(2)}, u32[]{:S(2)}) collective-permute-start(bf16[128,1024]{1,0:T(8,128)(2,1)} %get-tuple-element.131), channel_id=1, source_target_pairs={{0,4},{1,5},{2,6},{3,7},{4,0},{5,1},{6,2},{7,3},{8,12},{9,13},{10,... | collective-permute-start | bytes 786440 | tf_op jit(solution)/shard_map/ppermute | solution.py:111
  219.3 164.9 %reduce-scatter.4.cloned.1.call-start = ((), (), s32[]{:S(2)}) async-start(), calls=%async_computation.13 | async-start | bytes 4595712 | tf_op jit(solution)/shard_map/reduce_scatter | solution.py:592
  288.6 14.1 %collective-permute-start.23 = (bf16[128,3200]{1,0:T(8,128)(2,1)}, bf16[128,3200]{1,0:T(8,128)(2,1)S(1)}, u32[]{:S(2)}, u32[]{:S(2)}) collective-permute-start(bf16[128,3200]{1,0:T(8,128)(2,1)} %get-tuple-element.42.own), channel_id=1, source_target_pairs={{0,1},{1,0},{2,3},{3,2},{4,5},{5,4},{6,7},{7,6},{8,9},{9,8},{10,11... | collective-permute-start | bytes 2457608 | tf_op jit(solution)/shard_map/ppermute | solution.py:111
  317.0 23.3 %collective-permute-start.18 = (bf16[512,1024]{1,0:T(8,128)(2,1)S(1)}, bf16[512,1024]{1,0:T(8,128)(2,1)}, u32[]{:S(2)}, u32[]{:S(2)}) collective-permute-start(bf16[512,1024]{1,0:T(8,128)(2,1)S(1)} %slice.269), channel_id=1, source_target_pairs={{0,1},{1,0},{2,3},{3,2},{4,5},{5,4},{6,7},{7,6},{8,9},{9,8},{10,11... | collective-permute-start | bytes 3145736 | tf_op jit(solution)/shard_map/ppermute | solution.py:111
  336.6 13.2 %all-to-all-start.7 = ((bf16[8,32,768]{2,1,0:T(8,128)(2,1)}), bf16[8,32,768]{2,1,0:T(8,128)(2,1)S(1)}, u32[]{:S(2)}, u32[]{:S(2)}) async-start(bf16[8,32,768]{2,1,0:T(8,128)(2,1)} %bitcast.52), calls=%async_computation.9 | async-start | bytes 786432 | tf_op jit(solution)/shard_map/all_to_all | solution.py:509
  343.6 15.0 %collective-permute-start.19 = (bf16[128,1024]{1,0:T(8,128)(2,1)}, bf16[128,1024]{1,0:T(8,128)(2,1)}, u32[]{:S(2)}, u32[]{:S(2)}) collective-permute-start(bf16[128,1024]{1,0:T(8,128)(2,1)} %get-tuple-element.126), channel_id=1, source_target_pairs={{0,2},{1,3},{2,0},{3,1},{4,6},{5,7},{6,4},{7,5},{8,10},{9,11},{10,... | collective-permute-start | bytes 786440 | tf_op jit(solution)/shard_map/ppermute | solution.py:111
  345.3 14.4 %collective-permute-start.21 = (bf16[128,1024]{1,0:T(8,128)(2,1)}, bf16[128,1024]{1,0:T(8,128)(2,1)}, u32[]{:S(2)}, u32[]{:S(2)}) collective-permute-start(bf16[128,1024]{1,0:T(8,128)(2,1)} %get-tuple-element.127), channel_id=1, source_target_pairs={{0,6},{1,7},{2,4},{3,5},{4,2},{5,3},{6,0},{7,1},{8,14},{9,15},{10,... | collective-permute-start | bytes 786440 | tf_op jit(solution)/shard_map/ppermute | solution.py:111
  346.8 20.4 %collective-permute-start.20 = (bf16[128,1024]{1,0:T(8,128)(2,1)}, bf16[128,1024]{1,0:T(8,128)(2,1)}, u32[]{:S(2)}, u32[]{:S(2)}) collective-permute-start(bf16[128,1024]{1,0:T(8,128)(2,1)} %get-tuple-element.128), channel_id=1, source_target_pairs={{0,4},{1,5},{2,6},{3,7},{4,0},{5,1},{6,2},{7,3},{8,12},{9,13},{10,... | collective-permute-start | bytes 786440 | tf_op jit(solution)/shard_map/ppermute | solution.py:111
  (41 other events, 443.4 us)
Sparse Core Ops, SparseCore 0:
  13.8 81.1 all-gather.2
Sparse Core Ops, SparseCore 1:
  137.0 43.7 all-gather.4
  207.9 21.1 reduce-scatter.7
  231.2 39.0 reduce-scatter.5
  309.9 74.3 reduce-scatter.3
where the time goes:
time: 399 us; the launch traced here: 396 us
  waiting for transfers between devices  117 us (29%)
  blocking collectives  60.6 us (15%)
  local copies, waits for them, and re-layouts  56.1 us (14%)
  Pallas kernels  45.2 us (11%)
  starting transfers between devices  43.6 us (11%)
  matrix products  40.8 us (10%)
  other arithmetic  16.5 us (4%)
  between operations  16.3 us (4%)
    all_gather x1, waiting for transfers between devices, local(): first = lax.all_gather(first, 'seq', axis=0, tiled=True)  55.2 us
    all_to_all x2, blocking collectives, exchange(): return lax.all_to_all(array, 'seq', 0, 0)  36.8 us
    ppermute x26, waiting for transfers between devices, swapped(): lax.ppermute(array, 'seq', [(device, device ^ offset) for device in range...  25.2 us
    all_gather x1, blocking collectives, local(): lax.all_gather(w_down, 'seq', axis=0, tiled=True, axis_index_groups=columns)  23.8 us
    unnamed x78, local copies, waits for them, and re-layouts  22.7 us
    all_to_all x4, waiting for transfers between devices, exchange(): return lax.all_to_all(array, 'seq', 0, 0)  21.3 us
    all_to_all x4, starting transfers between devices, exchange(): return lax.all_to_all(array, 'seq', 0, 0)  19.1 us
    ppermute x26, starting transfers between devices, swapped(): lax.ppermute(array, 'seq', [(device, device ^ offset) for device in range...  16.8 us
  transfers between devices with their start and end apart: 37, of which 15 were waited for; matrix products, arithmetic and copies ran while one was open for 22% of the time, Pallas kernels for 11%

commit v1 on v0

--- a/solution.py
+++ b/solution.py
@@ -117,9 +117,17 @@
 
 
 def plane_scatter(partial):
+    return plane_scatter_rest(*plane_scatter_first(partial))
+
+
+def plane_scatter_first(partial):
     half = partial.shape[0] // 2
-    rows = half // len(OFFSETS)
-    joined = partial[:half] + swapped(partial[half:].astype(jnp.bfloat16), 1).astype(jnp.float32)
+    return partial[:half], partial[half:].astype(jnp.bfloat16)
+
+
+def plane_scatter_rest(kept, sent):
+    rows = kept.shape[0] // len(OFFSETS)
+    joined = kept + swapped(sent, 1).astype(jnp.float32)
     total = joined[:rows]
     for place, offset in enumerate(OFFSETS[1:], 1):
         piece = joined[place * rows : (place + 1) * rows].astype(jnp.bfloat16)
@@ -142,35 +150,16 @@
     return parts.transpose(1, 2, 0, 3).reshape(rows, hidden)
 
 
-def grad_body(left, own, other, *rest):
-    out = rest[-1]
-    tokens = own.shape[0]
-    total = outer_sum(left[:tokens, :], own[...]) + outer_sum(left[tokens:, :], other[...])
-    out[...] = total.astype(out.dtype)
-
-
-def grad_into(left, right, buffer, total, start, block):
-    tokens, height = left.shape
-    first = start // block
-    operands = [left, right, swapped(right, 1)]
-    specs = [
-        pl.BlockSpec((tokens, height), lambda j: (0, 0)),
-        pl.BlockSpec((tokens // 2, block), lambda j: (0, j)),
-        pl.BlockSpec((tokens // 2, block), lambda j: (0, j)),
-    ]
-    aliases = {}
-    if buffer is not None:
-        aliases = {len(operands): 0}
-        operands.append(buffer)
-        specs.append(pl.BlockSpec(memory_space=pl.ANY))
-    return pl.pallas_call(
-        grad_body,
-        grid=(pl.cdiv(right.shape[1], block),),
-        in_specs=specs,
-        out_specs=pl.BlockSpec((height, block), lambda j: (0, j + first)),
-        out_shape=jax.ShapeDtypeStruct((height, total), jnp.bfloat16),
-        input_output_aliases=aliases,
-    )(*operands)
+def grads_body(normed, own_first, other_first, gated, own_hidden, other_hidden, out):
+    tokens, start = own_first.shape[0], 0
+    for left, own, other in ((normed, own_first, other_first), (gated, own_hidden, other_hidden)):
+        for at in range(0, own.shape[1], 640):
+            width = min(640, own.shape[1] - at)
+            total = outer_sum(left[:tokens, :], own[:, at : at + width]) + outer_sum(
+                left[tokens:, :], other[:, at : at + width]
+            )
+            out[:, start + at : start + at + width] = total.astype(out.dtype)
+        start += own.shape[1]
 
 
 def with_partner(array):
@@ -356,13 +345,13 @@
         at_query = pl.multiple_of(head * width, width)
         at_key = pl.multiple_of((heads + head) * width, width)
         at_value = pl.multiple_of(2 * heads * width + head * value_width, value_width)
-        at_gate = pl.multiple_of(2 * heads * width + (heads + head) * value_width, value_width)
-        at_low = 2 * heads * (width + value_width)
+        at_low = heads * (2 * width + value_width)
+        at_gate = pl.multiple_of(at_low + LANES + head * value_width, LANES)
         out[at, pl.ds(at_query, width)] = (DK ** (-0.5) * d_query_in * rising).astype(out.dtype)
         out[at, pl.ds(at_key, width)] = (d_key_in * falling + d_key_end * fading).astype(out.dtype)
         out[at, pl.ds(at_value, value_width)] = d_values.astype(out.dtype)
         out[at, pl.ds(at_gate, value_width)] = d_gate[at, :]
-        out[at, at_low:] = d_low.astype(out.dtype)
+        out[at, at_low : at_low + LANES] = d_low.astype(out.dtype)
     bias_out[...] = bias_sum
 
 
@@ -410,15 +399,15 @@
             w_query,
             w_key,
             w_value,
-            w_outgate,
             jnp.pad(w_decay_down, ((0, 0), (0, LANES - rank))),
-            w_out,
         ],
         axis=1,
     )
     small = pack_small((w_decay_up, attn_gain, mlp_gain, decay_bias, head_gain))
     small = exchange(jnp.broadcast_to(small, (count, 1) + small.shape)).reshape(count, -1)
     first = lax.all_gather(first, "seq", axis=0, tiled=True)
+    second = jnp.concatenate([w_outgate, w_out], axis=1)
+    second = lax.all_gather(second, "seq", axis=0, tiled=True)
     levels = count // PLANE
     planes, columns = (plane_groups(count), level_groups(count))
     units = levels * w_down.shape[0]
@@ -426,30 +415,33 @@
     gate_up = jnp.concatenate([to_units(w_gate, levels, padded), to_units(w_up, levels, padded)], axis=2)
     gate_up = lax.all_to_all(gate_up, "seq", 0, 0, axis_index_groups=planes)
     gate_up = gate_up.reshape(PLANE * rows, 2 * padded)
+    gate_up, first = lax.optimization_barrier((gate_up, first))
     gate_up = lax.all_gather(gate_up, "seq", axis=0, tiled=True, axis_index_groups=columns)
     down = lax.all_gather(w_down, "seq", axis=0, tiled=True, axis_index_groups=columns)
     down = jnp.pad(down, ((0, padded - units), (0, 0)))
     cot_in, first = lax.optimization_barrier((cotangent.astype(jnp.bfloat16), first))
     cot_plane = plane_gather(cot_in)
-    widths = (key_width, key_width, value_width, value_width)
-    wide = 2 * key_width + 2 * value_width
-    projection = first[:, : wide + LANES]
+    wide = 2 * key_width + value_width
     up_pieces, attn_full, mlp_full_gain, bias_full, head_full = unpack_small(small, small_shapes)
     decay_up_full = up_pieces.transpose(1, 0, 2).reshape(rank, key_width)
     attn_full, mlp_full_gain, bias_full, head_full = (
         piece.reshape(-1).astype(jnp.float32) for piece in (attn_full, mlp_full_gain, bias_full, head_full)
     )
-    out_full = first[:, wide + LANES :]
     scaling = DK ** (-0.5)
     normed, norm_back = jax.vjp(rms_norm, block_input, attn_full)
     normed_in = normed.astype(jnp.bfloat16)
-    wide_out = matmul(normed_in, projection)
+    order = neighbour_ring(count)
+    chips = tuple(device // 2 for device in order[::2])
+    rings = [[2 * chip + core for chip in chips] for core in range(2)]
+    parity = lax.axis_index("seq") % 2
+    normed_pair = own_columns(with_partner(normed_in), chips, parity, rows)
+    normed_in, down, normed_pair = lax.optimization_barrier((normed_in, down, normed_pair))
+    wide_out = matmul(normed_in, first)
     tokens = wide_out.shape[0]
     up_rows = jnp.pad(decay_up_full, ((0, LANES - rank), (0, 0)))
     value_at = 2 * key_width // VALUE_WIDTH
     query_spec, key_spec = per_head(tokens, DK), per_head(tokens, DK, H)
     value_spec = per_head(tokens, VALUE_WIDTH, value_at)
-    gate_spec = per_head(tokens, VALUE_WIDTH, value_at + H)
     low_spec = whole_at(tokens, LANES, wide // LANES)
     up_spec = per_head(LANES, DK)
     head_values, head_keys = per_head(tokens, VALUE_WIDTH), per_head(tokens, DK)
@@ -471,16 +463,20 @@
     logs = arrived[:, :, VALUE_WIDTH:]
     before = exchange(scan_devices(prefix_body, arrived[:, :, :VALUE_WIDTH], logs))
     before = before.reshape(key_width, VALUE_WIDTH)
+    second, before = lax.optimization_barrier((second, before))
+    outgate_full, out_full = column_slices(second, (value_width, w_out.shape[1]))
+    outgate = matmul(normed_in, outgate_full)
     mixer, gated = pl.pallas_call(
         output_body,
         grid=(H,),
-        in_specs=[query_spec, key_spec, value_spec, head_keys, gate_spec, gain_spec, state_spec],
+        in_specs=[query_spec, key_spec, value_spec, head_keys, head_values, gain_spec, state_spec],
         out_specs=[head_values, head_values],
         out_shape=[
             jax.ShapeDtypeStruct((tokens, value_width), jnp.float32),
             jax.ShapeDtypeStruct((tokens, value_width), jnp.bfloat16),
         ],
-    )(wide_out, wide_out, wide_out, decay_logit, wide_out, gain_row, before)
+    )(wide_out, wide_out, wide_out, decay_logit, outgate, gain_row, before)
+    gated_pair = own_columns(with_partner(gated), chips, parity, rows)
     hidden_state = block_input + matmul(gated, out_full)
     mlp_full, mlp_back = jax.vjp(rms_norm, hidden_state, mlp_full_gain)
     mlp_normed = mlp_full.astype(jnp.bfloat16)
@@ -512,12 +508,13 @@
     sum_up_proj = from_units(sum_gate_up[:, :, padded:], levels, hidden)
     d_hidden_norm, grad_mlp_gain = mlp_back(d_mlp_normed)
     d_hidden = cotangent + d_hidden_norm
-    d_hidden_in = d_hidden.astype(jnp.bfloat16)
+    d_hidden_in, gated_pair = lax.optimization_barrier((d_hidden.astype(jnp.bfloat16), gated_pair))
+    hidden_other = swapped(d_hidden_in, 1)
     d_gated = times_back(d_hidden_in, out_full)
     mixer_gradient, d_outgate, grad_head_gain, state_gradient = pl.pallas_call(
         gate_back_body,
         grid=(H,),
-        in_specs=[head_values, head_values, gate_spec, gain_spec, query_spec, head_keys],
+        in_specs=[head_values, head_values, head_values, gain_spec, query_spec, head_keys],
         out_specs=[head_values, head_values, gain_spec, state_spec],
         out_shape=[
             jax.ShapeDtypeStruct((tokens, value_width), jnp.float32),
@@ -525,11 +522,13 @@
             jax.ShapeDtypeStruct((1, VALUE_WIDTH), jnp.float32),
             jax.ShapeDtypeStruct((key_width, VALUE_WIDTH), jnp.bfloat16),
         ],
-    )(d_gated, mixer, wide_out, gain_row, wide_out, decay_logit)
+    )(d_gated, mixer, outgate, gain_row, wide_out, decay_logit)
+    activ_late, state_gradient = lax.optimization_barrier((activ, state_gradient))
     arrived_back = exchange(state_gradient.reshape(count, chunk, VALUE_WIDTH))
     after = exchange(scan_devices(suffix_body, arrived_back, logs))
-    activ_late, after = lax.optimization_barrier((activ, after))
-    block_output = hidden_state + plane_scatter(matmul(activ_late, down))
+    kept, sent = plane_scatter_first(matmul(activ_late, down))
+    kept, sent, after = lax.optimization_barrier((kept, sent, after))
+    block_output = hidden_state + plane_scatter_rest(kept, sent)
     after = after.reshape(key_width, VALUE_WIDTH)
     d_first, d_logit_in, grad_decay_bias = pl.pallas_call(
         mixer_back_body,
@@ -545,9 +544,9 @@
             head_values,
             up_spec,
         ],
-        out_specs=[whole(tokens, wide + LANES), head_keys, per_head(1, DK)],
+        out_specs=[whole(tokens, wide + LANES + value_width), head_keys, per_head(1, DK)],
         out_shape=[
-            jax.ShapeDtypeStruct((tokens, wide + LANES), jnp.bfloat16),
+            jax.ShapeDtypeStruct((tokens, wide + LANES + value_width), jnp.bfloat16),
             jax.ShapeDtypeStruct((tokens, key_width), jnp.bfloat16),
             jax.ShapeDtypeStruct((1, key_width), jnp.float32),
         ],
@@ -565,7 +564,8 @@
     )
     low_rank = wide_out[:, wide : wide + rank].astype(jnp.bfloat16)
     grad_decay_up = outer_sum(low_rank, d_logit_in)
-    d_normed = times_back(d_first, projection)
+    d_normed = times_back(d_first[:, : wide + LANES], first)
+    d_normed = d_normed + times_back(d_first[:, wide + LANES :], outgate_full)
     d_input_norm, grad_attn_gain = norm_back(d_normed)
     input_grad = d_hidden + d_input_norm
 
@@ -580,22 +580,21 @@
         count,
     )
     small_sums = jnp.sum(exchange(small_sums), axis=0)
-    order = neighbour_ring(count)
-    chips = tuple(device // 2 for device in order[::2])
-    rings = [[2 * chip + core for chip in chips] for core in range(2)]
-    parity = lax.axis_index("seq") % 2
-    normed_pair = own_columns(with_partner(normed_in), chips, parity, rows)
-    gated_pair = own_columns(with_partner(gated), chips, parity, rows)
-    width = wide + LANES + w_out.shape[1]
-    sums = grad_into(gated_pair, d_hidden_in, None, width, wide + LANES, LANES)
-    sums = grad_into(normed_pair, d_first, sums, width, 0, 640)
+    sums = pl.pallas_call(
+        grads_body,
+        in_specs=[in_vmem()] * 6,
+        out_specs=in_vmem(),
+        out_shape=jax.ShapeDtypeStruct(
+            (normed_pair.shape[1], d_first.shape[1] + d_hidden_in.shape[1]), jnp.bfloat16
+        ),
+    )(normed_pair, d_first, swapped(d_first, 1), gated_pair, d_hidden_in, hidden_other)
     sums = lax.psum_scatter(
         sums, "seq", scatter_dimension=0, tiled=True, axis_index_groups=rings
     ).astype(jnp.float32)
-    sum_first, sum_out = column_slices(sums, (wide + LANES, w_out.shape[1]))
-    sum_query, sum_key, sum_value, sum_outgate, sum_decay_down = column_slices(
-        sum_first, widths + (rank,)
-    )
+    sum_query, sum_key, sum_value, sum_decay_down, sum_outgate, sum_out = column_slices(
+        sums, (key_width, key_width, value_width, LANES, value_width, w_out.shape[1])
+    )
+    sum_decay_down = sum_decay_down[:, :rank]
     sum_up, sum_attn, sum_mlp, sum_bias, sum_head = unpack_small(
         small_sums, small_shapes
     )

time: 399 us -> 373 us (0.935)
  blocking collectives: 60.6 us -> 41.7 us
  local copies, waits for them, and re-layouts: 56.1 us -> 49.2 us
  other arithmetic: 16.5 us -> 23.3 us
  Pallas kernels: 45.2 us -> 39.3 us
    all_gather x1, waiting for transfers between devices: 55.2 us -> 14.1 us  [local(): first = lax.all_gather(first, 'seq', axis=0, tiled=True)]
    all_gather x0 -> x1, waiting for transfers between devices: none -> 28.2 us  [local(): second = lax.all_gather(second, 'seq', axis=0, tiled=True)]
    all_to_all x2 -> x1, blocking collectives: 36.8 us -> 19.9 us  [exchange(): return lax.all_to_all(array, 'seq', 0, 0)]
    pallas_call x2 -> x1, Pallas kernels: 12 us -> 6.15 us  [local(): pl.pallas_call(grads_body, in_specs=[in_vmem()] * 6, out_specs=in_vmem(),...]
    unnamed x78 -> x77, local copies, waits for them, and re-layouts: 22.7 us -> 17.4 us
    ppermute x26, waiting for transfers between devices: 25.2 us -> 30.3 us  [swapped(): lax.ppermute(array, 'seq', [(device, device ^ offset) for device in range...]
    all_to_all x4 -> x5, waiting for transfers between devices: 21.3 us -> 25.9 us  [exchange(): return lax.all_to_all(array, 'seq', 0, 0)]
    dot_general x4 -> x5, matrix products: 12.6 us -> 14.5 us  [matmul(): return jnp.dot(left_side, right_side, preferred_element_type=jnp.float32)]
  transfers between devices with their start and end apart: 37 -> 39, of which waited for: 15 -> 15; matrix products, arithmetic and copies ran while one was open for 22% -> 25% of each run, Pallas kernels for 11% -> 11%
where the time goes in v1:
time: 373 us; the launch traced here: 371 us
  waiting for transfers between devices  120 us (32%)
  local copies, waits for them, and re-layouts  49.2 us (13%)
  starting transfers between devices  44.3 us (12%)
  blocking collectives  41.7 us (11%)
  Pallas kernels  39.3 us (11%)
  matrix products  38.6 us (10%)
  other arithmetic  23.3 us (6%)
  between operations  14.8 us (4%)
    ppermute x26, waiting for transfers between devices, swapped(): lax.ppermute(array, 'seq', [(device, device ^ offset) for device in range...  30.3 us
    all_gather x1, waiting for transfers between devices, local(): second = lax.all_gather(second, 'seq', axis=0, tiled=True)  28.2 us
    all_to_all x5, waiting for transfers between devices, exchange(): return lax.all_to_all(array, 'seq', 0, 0)  25.9 us
    all_gather x1, blocking collectives, local(): lax.all_gather(w_down, 'seq', axis=0, tiled=True, axis_index_groups=columns)  21.8 us
    all_to_all x1, blocking collectives, exchange(): return lax.all_to_all(array, 'seq', 0, 0)  19.9 us
    all_to_all x5, starting transfers between devices, exchange(): return lax.all_to_all(array, 'seq', 0, 0)  19.5 us
    unnamed x77, local copies, waits for them, and re-layouts  17.4 us
    ppermute x26, starting transfers between devices, swapped(): lax.ppermute(array, 'seq', [(device, device ^ offset) for device in range...  16.8 us
  transfers between devices with their start and end apart: 39, of which 15 were waited for; matrix products, arithmetic and copies ran while one was open for 25% of the time, Pallas kernels for 11%

profile of v1, /device:TPU:0, one launch (start us, length us, event | category | flops | bytes accessed | tf_op | source)
XLA Modules:
  0.0 371.2 jit_solution(16259556637707058967)
XLA Ops:
  16.8 7.3 %all-to-all-start = ((bf16[32,2,192]{2,1,0:T(2,128)(2,1)}), bf16[32,2,192]{2,1,0:T(2,128)(2,1)S(1)}, u32[]{:S(2)}, u32[]{:S(2)}) async-start(bf16[32,2,192]{2,1,0:T(2,128)(2,1)} %reshape.383), calls=%async_computation | async-start | bytes 65536 | tf_op jit(solution)/shard_map/all_to_all | solution.py:94
  28.4 21.8 %all_gather.12 = bf16[352,1024]{1,0:T(8,128)(2,1)S(1)} all-gather(bf16[88,1024]{1,0:T(8,128)(2,1)S(1)} %copy-done.16), channel_id=1, replica_groups={{0,8,16,24},{1,9,17,25},{2,10,18,26},{3,11,19,27},{4,12,20,28},{5,13,21..., dimensions={0}, use_global_device_ids=true | all-gather | bytes 901120 | tf_op jit(solution)/shard_map/all_gather | solution.py:420
  50.5 3.9 %all-to-all-start.1 = ((bf16[8,32,768]{2,1,0:T(8,128)(2,1)}), bf16[8,32,768]{2,1,0:T(8,128)(2,1)S(1)}, u32[]{:S(2)}, u32[]{:S(2)}) async-start(bf16[8,32,768]{2,1,0:T(8,128)(2,1)} %fusion.36), calls=%async_computation.1 | async-start | bytes 786432 | tf_op jit(solution)/shard_map/all_to_all | solution.py:416
  64.3 14.1 %all-gather.4.cloned.1.call-done = bf16[1024,2176]{1,0:T(8,128)(2,1)} async-done(((bf16[32,2176]{1,0:T(8,128)(2,1)}), bf16[1024,2176]{1,0:T(8,128)(2,1)}) %all-gather.4.cloned.1.call-update) | async-done | bytes 4456464 | tf_op jit(solution)/shard_map/all_gather | solution.py:408
  78.4 4.0 %fusion.64.key.value.low.query = f32[128,2176]{1,0:T(8,128)} fusion(bf16[128,1024]{1,0:T(8,128)(2,1)S(1)} %multiply_convert_fusion.3, bf16[1024,2176]{1,0:T(8,128)(2,1)} %all-gather.4.cloned.1.call-done), kind=kOutput, calls=%fused_computation.141 | convolution fusion | flops 570425344 | bytes 5832704 | tf_op jit(solution)/shard_map/dot_general | solution.py:179
  82.4 5.1 %shard_map.297 = (f32[128,512]{1,0:T(8,128)}, bf16[512,384]{1,0:T(8,128)(2,1)}) custom-call(f32[128,2176]{1,0:T(8,128)} %fusion.64.key.value.low.query, f32[128,2176]{1,0:T(8,128)} %fusion.64.key.value.low.query, f32[128,2176]{1,0:T(8,128)} %fusion.64.key.value.low.query, bf16[128,512]{1,0:T(8,128)(2,1)} %pad.32.up, f32[1,512]{1,0:T(1,128)} %reshape.287.bias), custom_call_target="tpu_custom_call" | custom-call | tf_op jit(solution)/shard_map/pallas_call | solution.py:452
  95.8 10.0 %all-to-all-done.2 = bf16[32,16,384]{2,1,0:T(8,128)(2,1)S(1)} async-done(((bf16[32,16,384]{2,1,0:T(8,128)(2,1)}), bf16[32,16,384]{2,1,0:T(8,128)(2,1)S(1)}, u32[]{:S(2)}, u32[]{:S(2)}) %all-to-all-start.2) | async-done | bytes 393248 | tf_op jit(solution)/shard_map/all_to_all | solution.py:94
  117.3 28.2 %all-gather.6.cloned.1.call-done = bf16[1024,2048]{1,0:T(8,128)(2,1)} async-done(((bf16[32,2048]{1,0:T(8,128)(2,1)}), bf16[1024,2048]{1,0:T(8,128)(2,1)}) %all-gather.6.cloned.1.call-update) | async-done | bytes 4194320 | tf_op jit(solution)/shard_map/all_gather | solution.py:410
  148.4 7.0 %shard_map.299 = (f32[128,1024]{1,0:T(8,128)}, bf16[128,1024]{1,0:T(8,128)(2,1)}) custom-call(f32[128,2176]{1,0:T(8,128)} %fusion.64.key.value.low.query, f32[128,2176]{1,0:T(8,128)} %fusion.64.key.value.low.query, f32[128,2176]{1,0:T(8,128)} %fusion.64.key.value.low.query, f32[128,512]{1,0:T(8,128)} %get-tuple-element.46.logit, f32[128,1024]{1,0:T(8,128)} %fusion.8.outgate, ...), custom_call_target="tpu_custom_call" | custom-call | tf_op jit(solution)/shard_map/pallas_call | solution.py:469
  168.6 4.8 %collective-permute-done.2 = bf16[128,1024]{1,0:T(8,128)(2,1)S(1)} collective-permute-done((bf16[128,1024]{1,0:T(8,128)(2,1)S(1)}, bf16[128,1024]{1,0:T(8,128)(2,1)S(1)}, u32[]{:S(2)}, u32[]{:S(2)}) %collective-permute-start.2) | collective-permute-done | bytes 262176 | tf_op jit(solution)/shard_map/ppermute | solution.py:111
  179.0 3.9 %all-gather.8.cloned.1.call-done = bf16[1024,768]{1,0:T(8,128)(2,1)} async-done(((bf16[256,768]{1,0:T(8,128)(2,1)}), bf16[1024,768]{1,0:T(8,128)(2,1)}) %all-gather.8.cloned.1.call-update) | async-done | bytes 1572880 | tf_op jit(solution)/shard_map/all_gather | solution.py:419
  183.0 4.1 %fusion.65 = f32[1024,768]{0,1:T(8,128)S(1)} fusion(bf16[1024,1024]{1,0:T(8,128)(2,1)} %constant_dynamic-update-slice_fusion, bf16[1024,768]{1,0:T(8,128)(2,1)} %all-gather.8.cloned.1.call-done), kind=kOutput, calls=%fused_computation.142 | convolution fusion | flops 1610612736 | bytes 6815744 | tf_op jit(solution)/shard_map/dot_general | solution.py:179
  200.8 4.6 %convolution_convert_fusion = bf16[1024,768]{1,0:T(8,128)(2,1)} fusion(bf16[1024,1024]{1,0:T(8,128)(2,1)} %constant_dynamic-update-slice_fusion, bf16[1024,384]{0,1:T(8,128)(2,1)S(1)} %copy-done.29, bf16[1024,384]{0,1:T(8,128)(2,1)S(1)} %copy-done.27), kind=kOutput, calls=%fused_computation.16 | convolution fusion | flops 1614544896 | bytes 5242880 | tf_op jit(solution)/shard_map/dot_general | solution.py:189
  207.8 5.1 %collective-permute-done.18 = bf16[128,1024]{1,0:T(8,128)(2,1)} collective-permute-done((bf16[128,1024]{1,0:T(8,128)(2,1)}, bf16[128,1024]{1,0:T(8,128)(2,1)}, u32[]{:S(2)}, u32[]{:S(2)}) %collective-permute-start.18) | collective-permute-done | bytes 262176 | tf_op jit(solution)/shard_map/ppermute | solution.py:111
  218.3 5.5 %shard_map.300 = (f32[128,1024]{1,0:T(8,128)}, bf16[128,1024]{1,0:T(8,128)(2,1)}, f32[1,256]{1,0:T(1,128)}, bf16[512,256]{1,0:T(8,128)(2,1)}) custom-call(f32[128,1024]{1,0:T(8,128)} %fusion.2.d_gated, f32[128,1024]{1,0:T(8,128)} %get-tuple-element.55.mixer, f32[128,1024]{1,0:T(8,128)} %fusion.8.outgate, f32[1,256]{1,0:T(1,128)} %reshape.288.gain, ...), custom_call_target="tpu_custom_call" | custom-call | tf_op jit(solution)/shard_map/pallas_call | solution.py:514
  223.8 19.9 %all_to_all.44.states = bf16[32,16,256]{2,1,0:T(8,128)(2,1)} all-to-all(bf16[32,16,256]{2,1,0:T(8,128)(2,1)} %bitcast.63), channel_id=1, replica_groups=mesh['seq'=32] {'seq'}, dimensions={0} | all-to-all | bytes 524288 | tf_op jit(solution)/shard_map/all_to_all | solution.py:94
  252.0 11.0 %all-to-all-done.5 = bf16[32,16,256]{2,1,0:T(8,128)(2,1)S(1)} async-done(((bf16[32,16,256]{2,1,0:T(8,128)(2,1)}), bf16[32,16,256]{2,1,0:T(8,128)(2,1)S(1)}, u32[]{:S(2)}, u32[]{:S(2)}) %all-to-all-start.5) | async-done | bytes 262176 | tf_op jit(solution)/shard_map/all_to_all | solution.py:94
  263.7 11.8 %shard_map.302 = (bf16[128,3200]{1,0:T(8,128)(2,1)}, bf16[128,512]{1,0:T(8,128)(2,1)}, f32[1,512]{1,0:T(1,128)}) custom-call(f32[128,2176]{1,0:T(8,128)} %fusion.64.key.value.low.query, f32[128,2176]{1,0:T(8,128)} %fusion.64.key.value.low.query, f32[128,2176]{1,0:T(8,128)} %fusion.64.key.value.low.query, f32[128,512]{1,0:T(8,128)} %get-tuple-element.46.logit, ...), custom_call_target="tpu_custom_call" | custom-call | tf_op jit(solution)/shard_map/pallas_call | solution.py:533
  279.2 6.2 %shard_map.303 = bf16[512,4224]{1,0:T(8,128)(2,1)} custom-call(bf16[256,512]{1,0:T(8,128)(2,1)} %fusion.1.normed, bf16[128,3200]{1,0:T(8,128)(2,1)} %get-tuple-element.64.own_first, bf16[128,3200]{1,0:T(8,128)(2,1)} %collective-permute-done.24.other_first, bf16[256,512]{1,0:T(8,128)(2,1)} %fusion.gated, bf16[128,1024]{1,0:T(8,128)(2,1)} %copy-done.12, ...), custom_call_target="tpu_custom_call" | custom-call | tf_op jit(solution)/shard_map/pallas_call | solution.py:583
  292.6 5.2 %multiply_reduce_fusion.1 = (f32[1024]{0:T(1024)S(1)}, f32[128]{0:T(128)}, f32[128,1024]{1,0:T(8,128)}) fusion(f32[128,1024]{1,0:T(8,128)S(1)} %copy-done, f32[128]{0:T(128)S(1)} %fusion.47, f32[1024]{0:T(1024)S(1)} %reshape.286, f32[128,1024]{1,0:T(8,128)S(1)} %fusion.6, bf16[1024,2176]{1,0:T(8,128)(2,1)} %all-gather.4.cloned.1.call-done, ...), kind=kOutput, calls=%fused_computation.56 | convolution fusion | flops 571341696 | bytes 6595584 | tf_op jit(solution)/shard_map/dot_general | solution.py:183
  307.6 5.0 %all-to-all-done.6 = f32[32,1,384]{2,1,0:T(1,128)S(1)} async-done(((f32[32,1,384]{2,1,0:T(1,128)}), f32[32,1,384]{2,1,0:T(1,128)S(1)}, u32[]{:S(2)}, u32[]{:S(2)}) %all-to-all-start.6) | async-done | bytes 49184 | tf_op jit(solution)/shard_map/all_to_all | solution.py:94
  329.4 6.3 %collective-permute-done.23 = bf16[128,1024]{1,0:T(8,128)(2,1)S(1)} collective-permute-done((bf16[128,1024]{1,0:T(8,128)(2,1)}, bf16[128,1024]{1,0:T(8,128)(2,1)S(1)}, u32[]{:S(2)}, u32[]{:S(2)}) %collective-permute-start.23) | collective-permute-done | bytes 262176 | tf_op jit(solution)/shard_map/ppermute | solution.py:111
  335.7 7.6 %collective-permute-done.22 = bf16[128,1024]{1,0:T(8,128)(2,1)S(1)} collective-permute-done((bf16[128,1024]{1,0:T(8,128)(2,1)S(1)}, bf16[128,1024]{1,0:T(8,128)(2,1)S(1)}, u32[]{:S(2)}, u32[]{:S(2)}) %collective-permute-start.22) | collective-permute-done | bytes 262176 | tf_op jit(solution)/shard_map/ppermute | solution.py:111
  345.4 14.5 %reduce-scatter.4.cloned.1.call-done = bf16[32,4224]{1,0:T(8,128)(2,1)} async-done(((bf16[512,4224]{1,0:T(8,128)(2,1)}), bf16[32,4224]{1,0:T(8,128)(2,1)}) %reduce-scatter.4.cloned.1.call-update) | async-done | bytes 270352 | tf_op jit(solution)/shard_map/reduce_scatter | solution.py:591
  (258 shorter events, 139.5 us)
Async XLA Ops:
  7.2 71.2 %all-gather.4.cloned.1.call-start = ((), (), s32[]{:S(2)}) async-start(), calls=%async_computation.11 | async-start | bytes 4595712 | tf_op jit(solution)/shard_map/all_gather | solution.py:408
  9.6 135.9 %all-gather.6.cloned.1.call-start = ((), (), s32[]{:S(2)}) async-start(), calls=%async_computation.12 | async-start | bytes 4325376 | tf_op jit(solution)/shard_map/all_gather | solution.py:410
  16.8 33.7 %all-to-all-start = ((bf16[32,2,192]{2,1,0:T(2,128)(2,1)}), bf16[32,2,192]{2,1,0:T(2,128)(2,1)S(1)}, u32[]{:S(2)}, u32[]{:S(2)}) async-start(bf16[32,2,192]{2,1,0:T(2,128)(2,1)} %reshape.383), calls=%async_computation | async-start | bytes 65536 | tf_op jit(solution)/shard_map/all_to_all | solution.py:94
  50.5 13.8 %all-to-all-start.1 = ((bf16[8,32,768]{2,1,0:T(8,128)(2,1)}), bf16[8,32,768]{2,1,0:T(8,128)(2,1)S(1)}, u32[]{:S(2)}, u32[]{:S(2)}) async-start(bf16[8,32,768]{2,1,0:T(8,128)(2,1)} %fusion.36), calls=%async_computation.1 | async-start | bytes 786432 | tf_op jit(solution)/shard_map/all_to_all | solution.py:416
  87.5 18.3 %all-to-all-start.2 = ((bf16[32,16,384]{2,1,0:T(8,128)(2,1)}), bf16[32,16,384]{2,1,0:T(8,128)(2,1)S(1)}, u32[]{:S(2)}, u32[]{:S(2)}) async-start(bf16[32,16,384]{2,1,0:T(8,128)(2,1)} %bitcast.57), calls=%async_computation.2 | async-start | bytes 786432 | tf_op jit(solution)/shard_map/all_to_all | solution.py:94
  90.7 21.9 %collective-permute-start.10 = (bf16[128,1024]{1,0:T(8,128)(2,1)S(1)}, bf16[128,1024]{1,0:T(8,128)(2,1)S(1)}, u32[]{:S(2)}, u32[]{:S(2)}) collective-permute-start(bf16[128,1024]{1,0:T(8,128)(2,1)S(1)} %convert_element_type.131), channel_id=1, source_target_pairs={{0,6},{1,7},{2,4},{3,5},{4,2},{5,3},{6,0},{7,1},{8,14},{9,15},{10,... | collective-permute-start | bytes 786440 | tf_op jit(solution)/shard_map/ppermute | solution.py:111
  93.4 19.5 %collective-permute-start.9 = (bf16[128,1024]{1,0:T(8,128)(2,1)S(1)}, bf16[128,1024]{1,0:T(8,128)(2,1)S(1)}, u32[]{:S(2)}, u32[]{:S(2)}) collective-permute-start(bf16[128,1024]{1,0:T(8,128)(2,1)S(1)} %convert_element_type.131), channel_id=1, source_target_pairs={{0,4},{1,5},{2,6},{3,7},{4,0},{5,1},{6,2},{7,3},{8,12},{9,13},{10,... | collective-permute-start | bytes 786440 | tf_op jit(solution)/shard_map/ppermute | solution.py:111
  94.0 19.2 %collective-permute-start.8 = (bf16[128,1024]{1,0:T(8,128)(2,1)S(1)}, bf16[128,1024]{1,0:T(8,128)(2,1)S(1)}, u32[]{:S(2)}, u32[]{:S(2)}) collective-permute-start(bf16[128,1024]{1,0:T(8,128)(2,1)S(1)} %convert_element_type.131), channel_id=1, source_target_pairs={{0,2},{1,3},{2,0},{3,1},{4,6},{5,7},{6,4},{7,5},{8,10},{9,11},{10,... | collective-permute-start | bytes 786440 | tf_op jit(solution)/shard_map/ppermute | solution.py:111
  95.8 19.8 %collective-permute-start.11 = (bf16[128,1024]{1,0:T(8,128)(2,1)S(1)}, bf16[128,1024]{1,0:T(8,128)(2,1)}, u32[]{:S(2)}, u32[]{:S(2)}) collective-permute-start(bf16[128,1024]{1,0:T(8,128)(2,1)S(1)} %convert_element_type.131), channel_id=1, source_target_pairs={{0,1},{1,0},{2,3},{3,2},{4,5},{5,4},{6,7},{7,6},{8,9},{9,8},{10,11... | collective-permute-start | bytes 786440 | tf_op jit(solution)/shard_map/ppermute | solution.py:111
  109.0 36.5 %all-to-all-start.3 = ((bf16[32,16,256]{2,1,0:T(8,128)(2,1)}), bf16[32,16,256]{2,1,0:T(8,128)(2,1)S(1)}, u32[]{:S(2)}, u32[]{:S(2)}) async-start(bf16[32,16,256]{2,1,0:T(8,128)(2,1)} %shard_map.298), calls=%async_computation.3 | async-start | bytes 524288 | tf_op jit(solution)/shard_map/all_to_all | solution.py:94
  111.6 71.3 %all-gather.8.cloned.1.call-start = ((), (), s32[]{:S(2)}) async-start(), calls=%async_computation.13 | async-start | bytes 1966080 | tf_op jit(solution)/shard_map/all_gather | solution.py:419
  112.4 175.0 %reduce-scatter.8.cloned.1.call-start = ((), (), s32[]{:S(2)}) async-start(), calls=%async_computation.16 | async-start | bytes 901120 | tf_op jit(solution)/shard_map/reduce_scatter | solution.py:495
  112.7 52.6 %collective-permute-start.14 = (bf16[128,1024]{1,0:T(8,128)(2,1)S(1)}, bf16[128,1024]{1,0:T(8,128)(2,1)S(1)}, u32[]{:S(2)}, u32[]{:S(2)}) collective-permute-start(bf16[128,1024]{1,0:T(8,128)(2,1)S(1)} %collective-permute-done.10), channel_id=1, source_target_pairs={{0,1},{1,0},{2,3},{3,2},{4,5},{5,4},{6,7},{7,6},{8,9},{9,8},{10,11... | collective-permute-start | bytes 786440 | tf_op jit(solution)/shard_map/ppermute | solution.py:111
  112.9 50.7 %collective-permute-start.13 = (bf16[128,1024]{1,0:T(8,128)(2,1)S(1)}, bf16[128,1024]{1,0:T(8,128)(2,1)}, u32[]{:S(2)}, u32[]{:S(2)}) collective-permute-start(bf16[128,1024]{1,0:T(8,128)(2,1)S(1)} %collective-permute-done.9), channel_id=1, source_target_pairs={{0,1},{1,0},{2,3},{3,2},{4,5},{5,4},{6,7},{7,6},{8,9},{9,8},{10,11... | collective-permute-start | bytes 786440 | tf_op jit(solution)/shard_map/ppermute | solution.py:111
  113.2 47.9 %collective-permute-start.12 = (bf16[128,1024]{1,0:T(8,128)(2,1)S(1)}, bf16[128,1024]{1,0:T(8,128)(2,1)}, u32[]{:S(2)}, u32[]{:S(2)}) collective-permute-start(bf16[128,1024]{1,0:T(8,128)(2,1)S(1)} %collective-permute-done.8), channel_id=1, source_target_pairs={{0,1},{1,0},{2,3},{3,2},{4,5},{5,4},{6,7},{7,6},{8,9},{9,8},{10,11... | collective-permute-start | bytes 786440 | tf_op jit(solution)/shard_map/ppermute | solution.py:111
  159.9 13.5 %collective-permute-start.2 = (bf16[128,1024]{1,0:T(8,128)(2,1)S(1)}, bf16[128,1024]{1,0:T(8,128)(2,1)S(1)}, u32[]{:S(2)}, u32[]{:S(2)}) collective-permute-start(bf16[128,1024]{1,0:T(8,128)(2,1)S(1)} %get-tuple-element.146), channel_id=1, source_target_pairs={{0,4},{1,5},{2,6},{3,7},{4,0},{5,1},{6,2},{7,3},{8,12},{9,13},{10,... | collective-permute-start | bytes 786440 | tf_op jit(solution)/shard_map/ppermute | solution.py:111
  193.6 119.1 %reduce-scatter.6.cloned.1.call-start = ((), (), s32[]{:S(2)}) async-start(), calls=%async_computation.15 | async-start | bytes 1966080 | tf_op jit(solution)/shard_map/reduce_scatter | solution.py:495
  198.7 14.2 %collective-permute-start.18 = (bf16[128,1024]{1,0:T(8,128)(2,1)}, bf16[128,1024]{1,0:T(8,128)(2,1)}, u32[]{:S(2)}, u32[]{:S(2)}) collective-permute-start(bf16[128,1024]{1,0:T(8,128)(2,1)} %get-tuple-element.154), channel_id=1, source_target_pairs={{0,6},{1,7},{2,4},{3,5},{4,2},{5,3},{6,0},{7,1},{8,14},{9,15},{10,... | collective-permute-start | bytes 786440 | tf_op jit(solution)/shard_map/ppermute | solution.py:111
  200.3 14.0 %collective-permute-start.17 = (bf16[128,1024]{1,0:T(8,128)(2,1)}, bf16[128,1024]{1,0:T(8,128)(2,1)}, u32[]{:S(2)}, u32[]{:S(2)}) collective-permute-start(bf16[128,1024]{1,0:T(8,128)(2,1)} %get-tuple-element.155), channel_id=1, source_target_pairs={{0,4},{1,5},{2,6},{3,7},{4,0},{5,1},{6,2},{7,3},{8,12},{9,13},{10,... | collective-permute-start | bytes 786440 | tf_op jit(solution)/shard_map/ppermute | solution.py:111
  245.6 17.3 %all-to-all-start.5 = ((bf16[32,16,256]{2,1,0:T(8,128)(2,1)}), bf16[32,16,256]{2,1,0:T(8,128)(2,1)S(1)}, u32[]{:S(2)}, u32[]{:S(2)}) async-start(bf16[32,16,256]{2,1,0:T(8,128)(2,1)} %shard_map.301), calls=%async_computation.5 | async-start | bytes 524288 | tf_op jit(solution)/shard_map/all_to_all | solution.py:94
  249.3 110.6 %reduce-scatter.4.cloned.1.call-start = ((), (), s32[]{:S(2)}) async-start(), calls=%async_computation.14 | async-start | bytes 4595712 | tf_op jit(solution)/shard_map/reduce_scatter | solution.py:591
  289.8 26.4 %collective-permute-start.20 = (bf16[512,1024]{1,0:T(8,128)(2,1)}, bf16[512,1024]{1,0:T(8,128)(2,1)}, u32[]{:S(2)}, u32[]{:S(2)}) collective-permute-start(bf16[512,1024]{1,0:T(8,128)(2,1)} %slice.276), channel_id=1, source_target_pairs={{0,1},{1,0},{2,3},{3,2},{4,5},{5,4},{6,7},{7,6},{8,9},{9,8},{10,11... | collective-permute-start | bytes 3145736 | tf_op jit(solution)/shard_map/ppermute | solution.py:111
  321.9 13.8 %collective-permute-start.23 = (bf16[128,1024]{1,0:T(8,128)(2,1)}, bf16[128,1024]{1,0:T(8,128)(2,1)S(1)}, u32[]{:S(2)}, u32[]{:S(2)}) collective-permute-start(bf16[128,1024]{1,0:T(8,128)(2,1)} %get-tuple-element.151), channel_id=1, source_target_pairs={{0,6},{1,7},{2,4},{3,5},{4,2},{5,3},{6,0},{7,1},{8,14},{9,15},{10,... | collective-permute-start | bytes 786440 | tf_op jit(solution)/shard_map/ppermute | solution.py:111
  323.4 20.0 %collective-permute-start.22 = (bf16[128,1024]{1,0:T(8,128)(2,1)S(1)}, bf16[128,1024]{1,0:T(8,128)(2,1)S(1)}, u32[]{:S(2)}, u32[]{:S(2)}) collective-permute-start(bf16[128,1024]{1,0:T(8,128)(2,1)S(1)} %get-tuple-element.152), channel_id=1, source_target_pairs={{0,4},{1,5},{2,6},{3,7},{4,0},{5,1},{6,2},{7,3},{8,12},{9,13},{10,... | collective-permute-start | bytes 786440 | tf_op jit(solution)/shard_map/ppermute | solution.py:111
  (45 other events, 962.9 us)
Sparse Core Ops, SparseCore 0:
  11.4 66.8 all-gather.3
  81.8 63.6 all-gather.5
  147.1 35.8 all-gather.7
  193.7 21.8 reduce-scatter.7
  217.7 39.6 reduce-scatter.5
  285.5 74.3 reduce-scatter.3

commit v2 on v1

--- a/solution.py
+++ b/solution.py
@@ -400,14 +400,14 @@
             w_key,
             w_value,
             jnp.pad(w_decay_down, ((0, 0), (0, LANES - rank))),
+            w_outgate,
         ],
         axis=1,
     )
     small = pack_small((w_decay_up, attn_gain, mlp_gain, decay_bias, head_gain))
     small = exchange(jnp.broadcast_to(small, (count, 1) + small.shape)).reshape(count, -1)
     first = lax.all_gather(first, "seq", axis=0, tiled=True)
-    second = jnp.concatenate([w_outgate, w_out], axis=1)
-    second = lax.all_gather(second, "seq", axis=0, tiled=True)
+    out_full = lax.all_gather(w_out, "seq", axis=0, tiled=True)
     levels = count // PLANE
     planes, columns = (plane_groups(count), level_groups(count))
     units = levels * w_down.shape[0]
@@ -436,7 +436,7 @@
     parity = lax.axis_index("seq") % 2
     normed_pair = own_columns(with_partner(normed_in), chips, parity, rows)
     normed_in, down, normed_pair = lax.optimization_barrier((normed_in, down, normed_pair))
-    wide_out = matmul(normed_in, first)
+    wide_out = matmul(normed_in, first[:, : wide + LANES])
     tokens = wide_out.shape[0]
     up_rows = jnp.pad(decay_up_full, ((0, LANES - rank), (0, 0)))
     value_at = 2 * key_width // VALUE_WIDTH
@@ -463,9 +463,7 @@
     logs = arrived[:, :, VALUE_WIDTH:]
     before = exchange(scan_devices(prefix_body, arrived[:, :, :VALUE_WIDTH], logs))
     before = before.reshape(key_width, VALUE_WIDTH)
-    second, before = lax.optimization_barrier((second, before))
-    outgate_full, out_full = column_slices(second, (value_width, w_out.shape[1]))
-    outgate = matmul(normed_in, outgate_full)
+    outgate = matmul(normed_in, first[:, wide + LANES :])
     mixer, gated = pl.pallas_call(
         output_body,
         grid=(H,),
@@ -564,8 +562,7 @@
     )
     low_rank = wide_out[:, wide : wide + rank].astype(jnp.bfloat16)
     grad_decay_up = outer_sum(low_rank, d_logit_in)
-    d_normed = times_back(d_first[:, : wide + LANES], first)
-    d_normed = d_normed + times_back(d_first[:, wide + LANES :], outgate_full)
+    d_normed = times_back(d_first, first)
     d_input_norm, grad_attn_gain = norm_back(d_normed)
     input_grad = d_hidden + d_input_norm
 

time: 373 us -> 374 us (level)
  other arithmetic: 23.3 us -> 18.9 us
  waiting for transfers between devices: 120 us -> 124 us
    all_gather x1, waiting for transfers between devices: 28.2 us -> 8.61 us  [local(): out_full = lax.all_gather(w_out, 'seq', axis=0, tiled=True)]
    all_gather x1, waiting for transfers between devices: 3.93 us -> 14 us  [local(): lax.all_gather(gate_up, 'seq', axis=0, tiled=True, axis_index_groups=colu...]
    all_gather x1, waiting for transfers between devices: 14.1 us -> 23.4 us  [local(): first = lax.all_gather(first, 'seq', axis=0, tiled=True)]
    dot_general x5 -> x4, matrix products: 12.9 us -> 11.3 us  [times_back(): lax.dot_general(left_side, right_side, (((1,), (1,)), ((), ())), preferre...]
    unnamed x77 -> x73, local copies, waits for them, and re-layouts: 17.4 us -> 19 us
  transfers between devices with their start and end apart: 39 -> 39, of which waited for: 15 -> 16; matrix products, arithmetic and copies ran while one was open for 25% -> 24% of each run, Pallas kernels for 11% -> 11%
where the time goes in v2:
time: 374 us; the launch traced here: 372 us
  waiting for transfers between devices  124 us (33%)
  local copies, waits for them, and re-layouts  51.5 us (14%)
  starting transfers between devices  44.8 us (12%)
  blocking collectives  41.6 us (11%)
  Pallas kernels  39.5 us (11%)
  matrix products  37.1 us (10%)
  other arithmetic  18.9 us (5%)
  between operations  14.8 us (4%)
    ppermute x26, waiting for transfers between devices, swapped(): lax.ppermute(array, 'seq', [(device, device ^ offset) for device in range...  30.3 us
    all_to_all x5, waiting for transfers between devices, exchange(): return lax.all_to_all(array, 'seq', 0, 0)  29.3 us
    all_gather x1, waiting for transfers between devices, local(): first = lax.all_gather(first, 'seq', axis=0, tiled=True)  23.4 us
    all_gather x1, blocking collectives, local(): lax.all_gather(w_down, 'seq', axis=0, tiled=True, axis_index_groups=columns)  21.6 us
    all_to_all x1, blocking collectives, exchange(): return lax.all_to_all(array, 'seq', 0, 0)  19.9 us
    all_to_all x5, starting transfers between devices, exchange(): return lax.all_to_all(array, 'seq', 0, 0)  19.8 us
    unnamed x73, local copies, waits for them, and re-layouts  19 us
    ppermute x26, starting transfers between devices, swapped(): lax.ppermute(array, 'seq', [(device, device ^ offset) for device in range...  17 us
  transfers between devices with their start and end apart: 39, of which 16 were waited for; matrix products, arithmetic and copies ran while one was open for 24% of the time, Pallas kernels for 11%

profile of v2, /device:TPU:0, one launch (start us, length us, event | category | flops | bytes accessed | tf_op | source)
XLA Modules:
  0.0 372.1 jit_solution(6427154610000587513)
XLA Ops:
  18.3 7.3 %all-to-all-start = ((bf16[32,2,192]{2,1,0:T(2,128)(2,1)}), bf16[32,2,192]{2,1,0:T(2,128)(2,1)S(1)}, u32[]{:S(2)}, u32[]{:S(2)}) async-start(bf16[32,2,192]{2,1,0:T(2,128)(2,1)} %reshape.383), calls=%async_computation | async-start | bytes 65536 | tf_op jit(solution)/shard_map/all_to_all | solution.py:94
  29.4 21.6 %all_gather.12 = bf16[352,1024]{1,0:T(8,128)(2,1)S(1)} all-gather(bf16[88,1024]{1,0:T(8,128)(2,1)S(1)} %copy-done.16), channel_id=1, replica_groups={{0,8,16,24},{1,9,17,25},{2,10,18,26},{3,11,19,27},{4,12,20,28},{5,13,21..., dimensions={0}, use_global_device_ids=true | all-gather | bytes 901120 | tf_op jit(solution)/shard_map/all_gather | solution.py:420
  63.4 23.4 %all-gather.4.cloned.1.call-done = bf16[1024,3200]{1,0:T(8,128)(2,1)} async-done(((bf16[32,3200]{1,0:T(8,128)(2,1)}), bf16[1024,3200]{1,0:T(8,128)(2,1)}) %all-gather.4.cloned.1.call-update) | async-done | bytes 6553616 | tf_op jit(solution)/shard_map/all_gather | solution.py:409
  86.8 4.2 %fusion.key.value.low.query = f32[128,2176]{1,0:T(8,128)} fusion(bf16[128,1024]{1,0:T(8,128)(2,1)} %multiply_convert_fusion.3, bf16[1024,3200]{1,0:T(8,128)(2,1)} %all-gather.4.cloned.1.call-done), kind=kOutput, calls=%fused_computation | convolution fusion | flops 570425344 | bytes 5832704 | tf_op jit(solution)/shard_map/dot_general | solution.py:179
  91.0 5.1 %shard_map.297 = (f32[128,512]{1,0:T(8,128)}, bf16[512,384]{1,0:T(8,128)(2,1)}) custom-call(f32[128,2176]{1,0:T(8,128)} %fusion.key.value.low.query, f32[128,2176]{1,0:T(8,128)} %fusion.key.value.low.query, f32[128,2176]{1,0:T(8,128)} %fusion.key.value.low.query, bf16[128,512]{1,0:T(8,128)(2,1)} %pad.32.up, f32[1,512]{1,0:T(1,128)} %reshape.287.bias), custom_call_target="tpu_custom_call" | custom-call | tf_op jit(solution)/shard_map/pallas_call | solution.py:452
  106.7 6.5 %all-to-all-done.2 = bf16[32,16,384]{2,1,0:T(8,128)(2,1)S(1)} async-done(((bf16[32,16,384]{2,1,0:T(8,128)(2,1)}), bf16[32,16,384]{2,1,0:T(8,128)(2,1)S(1)}, u32[]{:S(2)}, u32[]{:S(2)}) %all-to-all-start.2) | async-done | bytes 393248 | tf_op jit(solution)/shard_map/all_to_all | solution.py:94
  123.9 6.6 %all-to-all-done.3 = bf16[32,16,256]{2,1,0:T(8,128)(2,1)S(1)} async-done(((bf16[32,16,256]{2,1,0:T(8,128)(2,1)}), bf16[32,16,256]{2,1,0:T(8,128)(2,1)S(1)}, u32[]{:S(2)}, u32[]{:S(2)}) %all-to-all-start.3) | async-done | bytes 262176 | tf_op jit(solution)/shard_map/all_to_all | solution.py:94
  131.2 7.1 %shard_map.299 = (f32[128,1024]{1,0:T(8,128)}, bf16[128,1024]{1,0:T(8,128)(2,1)}) custom-call(f32[128,2176]{1,0:T(8,128)} %fusion.key.value.low.query, f32[128,2176]{1,0:T(8,128)} %fusion.key.value.low.query, f32[128,2176]{1,0:T(8,128)} %fusion.key.value.low.query, f32[128,512]{1,0:T(8,128)} %get-tuple-element.44.logit, f32[128,1024]{1,0:T(8,128)} %fusion.2.outgate, ...), custom_call_target="tpu_custom_call" | custom-call | tf_op jit(solution)/shard_map/pallas_call | solution.py:467
  138.4 8.6 %all-gather.6.cloned.1.call-done = bf16[1024,1024]{1,0:T(8,128)(2,1)} async-done(((bf16[32,1024]{1,0:T(8,128)(2,1)}), bf16[1024,1024]{1,0:T(8,128)(2,1)}) %all-gather.6.cloned.1.call-update) | async-done | bytes 2097168 | tf_op jit(solution)/shard_map/all_gather | solution.py:410
  160.2 4.8 %collective-permute-done.2 = bf16[128,1024]{1,0:T(8,128)(2,1)S(1)} collective-permute-done((bf16[128,1024]{1,0:T(8,128)(2,1)S(1)}, bf16[128,1024]{1,0:T(8,128)(2,1)S(1)}, u32[]{:S(2)}, u32[]{:S(2)}) %collective-permute-start.2) | collective-permute-done | bytes 262176 | tf_op jit(solution)/shard_map/ppermute | solution.py:111
  170.6 14.0 %all-gather.8.cloned.1.call-done = bf16[1024,768]{1,0:T(8,128)(2,1)} async-done(((bf16[256,768]{1,0:T(8,128)(2,1)}), bf16[1024,768]{1,0:T(8,128)(2,1)}) %all-gather.8.cloned.1.call-update) | async-done | bytes 1572880 | tf_op jit(solution)/shard_map/all_gather | solution.py:419
  184.5 4.1 %fusion.53 = f32[1024,768]{0,1:T(8,128)S(1)} fusion(bf16[1024,1024]{1,0:T(8,128)(2,1)} %constant_dynamic-update-slice_fusion.5, bf16[1024,768]{1,0:T(8,128)(2,1)} %all-gather.8.cloned.1.call-done), kind=kOutput, calls=%fused_computation.135 | convolution fusion | flops 1610612736 | bytes 6815744 | tf_op jit(solution)/shard_map/dot_general | solution.py:179
  202.4 4.6 %convolution_convert_fusion = bf16[1024,768]{1,0:T(8,128)(2,1)} fusion(bf16[1024,1024]{1,0:T(8,128)(2,1)} %constant_dynamic-update-slice_fusion.5, bf16[1024,384]{0,1:T(8,128)(2,1)S(1)} %copy-done.25, bf16[1024,384]{0,1:T(8,128)(2,1)S(1)} %copy-done.23), kind=kOutput, calls=%fused_computation.12 | convolution fusion | flops 1614544896 | bytes 5242880 | tf_op jit(solution)/shard_map/dot_general | solution.py:189
  209.4 5.2 %collective-permute-done.18 = bf16[128,1024]{1,0:T(8,128)(2,1)} collective-permute-done((bf16[128,1024]{1,0:T(8,128)(2,1)}, bf16[128,1024]{1,0:T(8,128)(2,1)}, u32[]{:S(2)}, u32[]{:S(2)}) %collective-permute-start.18) | collective-permute-done | bytes 262176 | tf_op jit(solution)/shard_map/ppermute | solution.py:111
  220.0 5.5 %shard_map.300 = (f32[128,1024]{1,0:T(8,128)}, bf16[128,1024]{1,0:T(8,128)(2,1)}, f32[1,256]{1,0:T(1,128)}, bf16[512,256]{1,0:T(8,128)(2,1)}) custom-call(f32[128,1024]{1,0:T(8,128)} %fusion.54.d_gated, f32[128,1024]{1,0:T(8,128)} %get-tuple-element.51.mixer, f32[128,1024]{1,0:T(8,128)} %fusion.2.outgate, f32[1,256]{1,0:T(1,128)} %reshape.288.gain, ...), custom_call_target="tpu_custom_call" | custom-call | tf_op jit(solution)/shard_map/pallas_call | solution.py:512
  225.5 19.9 %all_to_all.44.states = bf16[32,16,256]{2,1,0:T(8,128)(2,1)} all-to-all(bf16[32,16,256]{2,1,0:T(8,128)(2,1)} %bitcast.64), channel_id=1, replica_groups=mesh['seq'=32] {'seq'}, dimensions={0} | all-to-all | bytes 524288 | tf_op jit(solution)/shard_map/all_to_all | solution.py:94
  254.1 10.7 %all-to-all-done.5 = bf16[32,16,256]{2,1,0:T(8,128)(2,1)} async-done(((bf16[32,16,256]{2,1,0:T(8,128)(2,1)}), bf16[32,16,256]{2,1,0:T(8,128)(2,1)}, u32[]{:S(2)}, u32[]{:S(2)}) %all-to-all-start.5) | async-done | bytes 262176 | tf_op jit(solution)/shard_map/all_to_all | solution.py:94
  264.8 11.9 %shard_map.302 = (bf16[128,3200]{1,0:T(8,128)(2,1)}, bf16[128,512]{1,0:T(8,128)(2,1)}, f32[1,512]{1,0:T(1,128)}) custom-call(f32[128,2176]{1,0:T(8,128)} %fusion.key.value.low.query, f32[128,2176]{1,0:T(8,128)} %fusion.key.value.low.query, f32[128,2176]{1,0:T(8,128)} %fusion.key.value.low.query, f32[128,512]{1,0:T(8,128)} %get-tuple-element.44.logit, ...), custom_call_target="tpu_custom_call" | custom-call | tf_op jit(solution)/shard_map/pallas_call | solution.py:531
  280.3 6.2 %shard_map.303 = bf16[512,4224]{1,0:T(8,128)(2,1)} custom-call(bf16[256,512]{1,0:T(8,128)(2,1)} %fusion.5.normed, bf16[128,3200]{1,0:T(8,128)(2,1)} %get-tuple-element.60.own_first, bf16[128,3200]{1,0:T(8,128)(2,1)} %collective-permute-done.24.other_first, bf16[256,512]{1,0:T(8,128)(2,1)} %fusion.4.gated, bf16[128,1024]{1,0:T(8,128)(2,1)} %copy-done.6, ...), custom_call_target="tpu_custom_call" | custom-call | tf_op jit(solution)/shard_map/pallas_call | solution.py:580
  291.7 6.1 %multiply_reduce_fusion.1 = (f32[1024]{0:T(1024)S(1)}, f32[128]{0:T(128)S(1)}, f32[128,1024]{1,0:T(8,128)}) fusion(f32[128,1024]{1,0:T(8,128)S(1)} %copy-done, f32[128]{0:T(128)S(1)} %fusion.36, f32[1024]{0:T(1024)S(1)} %reshape.286, bf16[128,3200]{1,0:T(8,128)(2,1)} %get-tuple-element.60.own_first, bf16[1024,3200]{1,0:T(8,128)(2,1)} %all-gather.4.cloned.1.call-done), kind=kOutput, calls=%fused_computation.50 | convolution fusion | flops 839646080 | bytes 8430592 | tf_op jit(solution)/shard_map/dot_general | solution.py:183
  307.2 5.5 %all-to-all-done.6 = f32[32,1,384]{2,1,0:T(1,128)S(1)} async-done(((f32[32,1,384]{2,1,0:T(1,128)}), f32[32,1,384]{2,1,0:T(1,128)S(1)}, u32[]{:S(2)}, u32[]{:S(2)}) %all-to-all-start.6) | async-done | bytes 49184 | tf_op jit(solution)/shard_map/all_to_all | solution.py:94
  329.6 6.3 %collective-permute-done.23 = bf16[128,1024]{1,0:T(8,128)(2,1)S(1)} collective-permute-done((bf16[128,1024]{1,0:T(8,128)(2,1)}, bf16[128,1024]{1,0:T(8,128)(2,1)S(1)}, u32[]{:S(2)}, u32[]{:S(2)}) %collective-permute-start.23) | collective-permute-done | bytes 262176 | tf_op jit(solution)/shard_map/ppermute | solution.py:111
  335.9 7.6 %collective-permute-done.22 = bf16[128,1024]{1,0:T(8,128)(2,1)S(1)} collective-permute-done((bf16[128,1024]{1,0:T(8,128)(2,1)S(1)}, bf16[128,1024]{1,0:T(8,128)(2,1)S(1)}, u32[]{:S(2)}, u32[]{:S(2)}) %collective-permute-start.22) | collective-permute-done | bytes 262176 | tf_op jit(solution)/shard_map/ppermute | solution.py:111
  345.5 15.3 %reduce-scatter.4.cloned.1.call-done = bf16[32,4224]{1,0:T(8,128)(2,1)} async-done(((bf16[512,4224]{1,0:T(8,128)(2,1)}), bf16[32,4224]{1,0:T(8,128)(2,1)}) %reduce-scatter.4.cloned.1.call-update) | async-done | bytes 270352 | tf_op jit(solution)/shard_map/reduce_scatter | solution.py:588
  (252 shorter events, 139.1 us)
Async XLA Ops:
  7.2 79.6 %all-gather.4.cloned.1.call-start = ((), (), s32[]{:S(2)}) async-start(), calls=%async_computation.11 | async-start | bytes 6758400 | tf_op jit(solution)/shard_map/all_gather | solution.py:409
  12.0 135.0 %all-gather.6.cloned.1.call-start = ((), (), s32[]{:S(2)}) async-start(), calls=%async_computation.12 | async-start | bytes 2162688 | tf_op jit(solution)/shard_map/all_gather | solution.py:410
  18.3 33.1 %all-to-all-start = ((bf16[32,2,192]{2,1,0:T(2,128)(2,1)}), bf16[32,2,192]{2,1,0:T(2,128)(2,1)S(1)}, u32[]{:S(2)}, u32[]{:S(2)}) async-start(bf16[32,2,192]{2,1,0:T(2,128)(2,1)} %reshape.383), calls=%async_computation | async-start | bytes 65536 | tf_op jit(solution)/shard_map/all_to_all | solution.py:94
  96.1 17.2 %all-to-all-start.2 = ((bf16[32,16,384]{2,1,0:T(8,128)(2,1)}), bf16[32,16,384]{2,1,0:T(8,128)(2,1)S(1)}, u32[]{:S(2)}, u32[]{:S(2)}) async-start(bf16[32,16,384]{2,1,0:T(8,128)(2,1)} %bitcast.58), calls=%async_computation.2 | async-start | bytes 786432 | tf_op jit(solution)/shard_map/all_to_all | solution.py:94
  100.1 23.1 %collective-permute-start.11 = (bf16[128,1024]{1,0:T(8,128)(2,1)S(1)}, bf16[128,1024]{1,0:T(8,128)(2,1)S(1)}, u32[]{:S(2)}, u32[]{:S(2)}) collective-permute-start(bf16[128,1024]{1,0:T(8,128)(2,1)S(1)} %convert_element_type.131), channel_id=1, source_target_pairs={{0,1},{1,0},{2,3},{3,2},{4,5},{5,4},{6,7},{7,6},{8,9},{9,8},{10,11... | collective-permute-start | bytes 786440 | tf_op jit(solution)/shard_map/ppermute | solution.py:111
  100.3 19.8 %collective-permute-start.10 = (bf16[128,1024]{1,0:T(8,128)(2,1)S(1)}, bf16[128,1024]{1,0:T(8,128)(2,1)S(1)}, u32[]{:S(2)}, u32[]{:S(2)}) collective-permute-start(bf16[128,1024]{1,0:T(8,128)(2,1)S(1)} %convert_element_type.131), channel_id=1, source_target_pairs={{0,6},{1,7},{2,4},{3,5},{4,2},{5,3},{6,0},{7,1},{8,14},{9,15},{10,... | collective-permute-start | bytes 786440 | tf_op jit(solution)/shard_map/ppermute | solution.py:111
  102.8 17.6 %collective-permute-start.9 = (bf16[128,1024]{1,0:T(8,128)(2,1)S(1)}, bf16[128,1024]{1,0:T(8,128)(2,1)S(1)}, u32[]{:S(2)}, u32[]{:S(2)}) collective-permute-start(bf16[128,1024]{1,0:T(8,128)(2,1)S(1)} %convert_element_type.131), channel_id=1, source_target_pairs={{0,4},{1,5},{2,6},{3,7},{4,0},{5,1},{6,2},{7,3},{8,12},{9,13},{10,... | collective-permute-start | bytes 786440 | tf_op jit(solution)/shard_map/ppermute | solution.py:111
  103.4 17.3 %collective-permute-start.8 = (bf16[128,1024]{1,0:T(8,128)(2,1)S(1)}, bf16[128,1024]{1,0:T(8,128)(2,1)S(1)}, u32[]{:S(2)}, u32[]{:S(2)}) collective-permute-start(bf16[128,1024]{1,0:T(8,128)(2,1)S(1)} %convert_element_type.131), channel_id=1, source_target_pairs={{0,2},{1,3},{2,0},{3,1},{4,6},{5,7},{6,4},{7,5},{8,10},{9,11},{10,... | collective-permute-start | bytes 786440 | tf_op jit(solution)/shard_map/ppermute | solution.py:111
  116.5 14.1 %all-to-all-start.3 = ((bf16[32,16,256]{2,1,0:T(8,128)(2,1)}), bf16[32,16,256]{2,1,0:T(8,128)(2,1)S(1)}, u32[]{:S(2)}, u32[]{:S(2)}) async-start(bf16[32,16,256]{2,1,0:T(8,128)(2,1)} %shard_map.298), calls=%async_computation.3 | async-start | bytes 524288 | tf_op jit(solution)/shard_map/all_to_all | solution.py:94
  119.1 65.4 %all-gather.8.cloned.1.call-start = ((), (), s32[]{:S(2)}) async-start(), calls=%async_computation.13 | async-start | bytes 1966080 | tf_op jit(solution)/shard_map/all_gather | solution.py:419
  119.9 169.2 %reduce-scatter.8.cloned.1.call-start = ((), (), s32[]{:S(2)}) async-start(), calls=%async_computation.16 | async-start | bytes 901120 | tf_op jit(solution)/shard_map/reduce_scatter | solution.py:493
  120.2 36.8 %collective-permute-start.14 = (bf16[128,1024]{1,0:T(8,128)(2,1)S(1)}, bf16[128,1024]{1,0:T(8,128)(2,1)S(1)}, u32[]{:S(2)}, u32[]{:S(2)}) collective-permute-start(bf16[128,1024]{1,0:T(8,128)(2,1)S(1)} %collective-permute-done.10), channel_id=1, source_target_pairs={{0,1},{1,0},{2,3},{3,2},{4,5},{5,4},{6,7},{7,6},{8,9},{9,8},{10,11... | collective-permute-start | bytes 786440 | tf_op jit(solution)/shard_map/ppermute | solution.py:111
  120.5 34.8 %collective-permute-start.13 = (bf16[128,1024]{1,0:T(8,128)(2,1)S(1)}, bf16[128,1024]{1,0:T(8,128)(2,1)}, u32[]{:S(2)}, u32[]{:S(2)}) collective-permute-start(bf16[128,1024]{1,0:T(8,128)(2,1)S(1)} %collective-permute-done.9), channel_id=1, source_target_pairs={{0,1},{1,0},{2,3},{3,2},{4,5},{5,4},{6,7},{7,6},{8,9},{9,8},{10,11... | collective-permute-start | bytes 786440 | tf_op jit(solution)/shard_map/ppermute | solution.py:111
  120.7 32.3 %collective-permute-start.12 = (bf16[128,1024]{1,0:T(8,128)(2,1)S(1)}, bf16[128,1024]{1,0:T(8,128)(2,1)}, u32[]{:S(2)}, u32[]{:S(2)}) collective-permute-start(bf16[128,1024]{1,0:T(8,128)(2,1)S(1)} %collective-permute-done.8), channel_id=1, source_target_pairs={{0,1},{1,0},{2,3},{3,2},{4,5},{5,4},{6,7},{7,6},{8,9},{9,8},{10,11... | collective-permute-start | bytes 786440 | tf_op jit(solution)/shard_map/ppermute | solution.py:111
  151.5 13.5 %collective-permute-start.2 = (bf16[128,1024]{1,0:T(8,128)(2,1)S(1)}, bf16[128,1024]{1,0:T(8,128)(2,1)S(1)}, u32[]{:S(2)}, u32[]{:S(2)}) collective-permute-start(bf16[128,1024]{1,0:T(8,128)(2,1)S(1)} %get-tuple-element.142), channel_id=1, source_target_pairs={{0,4},{1,5},{2,6},{3,7},{4,0},{5,1},{6,2},{7,3},{8,12},{9,13},{10,... | collective-permute-start | bytes 786440 | tf_op jit(solution)/shard_map/ppermute | solution.py:111
  195.2 117.6 %reduce-scatter.6.cloned.1.call-start = ((), (), s32[]{:S(2)}) async-start(), calls=%async_computation.15 | async-start | bytes 1966080 | tf_op jit(solution)/shard_map/reduce_scatter | solution.py:493
  200.4 14.1 %collective-permute-start.18 = (bf16[128,1024]{1,0:T(8,128)(2,1)}, bf16[128,1024]{1,0:T(8,128)(2,1)}, u32[]{:S(2)}, u32[]{:S(2)}) collective-permute-start(bf16[128,1024]{1,0:T(8,128)(2,1)} %get-tuple-element.150), channel_id=1, source_target_pairs={{0,6},{1,7},{2,4},{3,5},{4,2},{5,3},{6,0},{7,1},{8,14},{9,15},{10,... | collective-permute-start | bytes 786440 | tf_op jit(solution)/shard_map/ppermute | solution.py:111
  201.9 14.0 %collective-permute-start.17 = (bf16[128,1024]{1,0:T(8,128)(2,1)}, bf16[128,1024]{1,0:T(8,128)(2,1)}, u32[]{:S(2)}, u32[]{:S(2)}) collective-permute-start(bf16[128,1024]{1,0:T(8,128)(2,1)} %get-tuple-element.151), channel_id=1, source_target_pairs={{0,4},{1,5},{2,6},{3,7},{4,0},{5,1},{6,2},{7,3},{8,12},{9,13},{10,... | collective-permute-start | bytes 786440 | tf_op jit(solution)/shard_map/ppermute | solution.py:111
  247.3 17.5 %all-to-all-start.5 = ((bf16[32,16,256]{2,1,0:T(8,128)(2,1)}), bf16[32,16,256]{2,1,0:T(8,128)(2,1)}, u32[]{:S(2)}, u32[]{:S(2)}) async-start(bf16[32,16,256]{2,1,0:T(8,128)(2,1)} %shard_map.301), calls=%async_computation.5 | async-start | bytes 524288 | tf_op jit(solution)/shard_map/all_to_all | solution.py:94
  251.1 109.7 %reduce-scatter.4.cloned.1.call-start = ((), (), s32[]{:S(2)}) async-start(), calls=%async_computation.14 | async-start | bytes 4595712 | tf_op jit(solution)/shard_map/reduce_scatter | solution.py:588
  291.5 24.8 %collective-permute-start.20 = (bf16[512,1024]{1,0:T(8,128)(2,1)}, bf16[512,1024]{1,0:T(8,128)(2,1)}, u32[]{:S(2)}, u32[]{:S(2)}) collective-permute-start(bf16[512,1024]{1,0:T(8,128)(2,1)} %slice.258), channel_id=1, source_target_pairs={{0,1},{1,0},{2,3},{3,2},{4,5},{5,4},{6,7},{7,6},{8,9},{9,8},{10,11... | collective-permute-start | bytes 3145736 | tf_op jit(solution)/shard_map/ppermute | solution.py:111
  312.8 13.3 %all-to-all-start.7 = ((bf16[8,32,768]{2,1,0:T(8,128)(2,1)}), bf16[8,32,768]{2,1,0:T(8,128)(2,1)S(1)}, u32[]{:S(2)}, u32[]{:S(2)}) async-start(bf16[8,32,768]{2,1,0:T(8,128)(2,1)} %bitcast.57), calls=%async_computation.9 | async-start | bytes 786432 | tf_op jit(solution)/shard_map/all_to_all | solution.py:503
  322.1 13.8 %collective-permute-start.23 = (bf16[128,1024]{1,0:T(8,128)(2,1)}, bf16[128,1024]{1,0:T(8,128)(2,1)S(1)}, u32[]{:S(2)}, u32[]{:S(2)}) collective-permute-start(bf16[128,1024]{1,0:T(8,128)(2,1)} %get-tuple-element.147), channel_id=1, source_target_pairs={{0,6},{1,7},{2,4},{3,5},{4,2},{5,3},{6,0},{7,1},{8,14},{9,15},{10,... | collective-permute-start | bytes 786440 | tf_op jit(solution)/shard_map/ppermute | solution.py:111
  323.6 20.0 %collective-permute-start.22 = (bf16[128,1024]{1,0:T(8,128)(2,1)S(1)}, bf16[128,1024]{1,0:T(8,128)(2,1)S(1)}, u32[]{:S(2)}, u32[]{:S(2)}) collective-permute-start(bf16[128,1024]{1,0:T(8,128)(2,1)S(1)} %get-tuple-element.148), channel_id=1, source_target_pairs={{0,4},{1,5},{2,6},{3,7},{4,0},{5,1},{6,2},{7,3},{8,12},{9,13},{10,... | collective-permute-start | bytes 786440 | tf_op jit(solution)/shard_map/ppermute | solution.py:111
  (41 other events, 523.3 us)
Sparse Core Ops, SparseCore 0:
  12.1 74.6 all-gather.3
  89.6 57.3 all-gather.5
  148.6 35.9 all-gather.7
  195.3 21.8 reduce-scatter.7
  219.4 39.6 reduce-scatter.5
  286.7 74.0 reduce-scatter.3
